TPU v7x, 32 devices: a whole 2x2x4 slice. The times are simulated.
32 devices in a mesh: groups: 2 (over y), ctx: 16 (over z, x, core).
Axes of the slice: x: 2, y: 2, z: 4, core: 2. Of those that a mesh axis runs over, the one named last changes fastest.
Arguments:
- query_rows: bfloat16 [4096, 2560], P(('groups', 'ctx')), parts along dimension 0, may hold values from -211 to 211
- key_rows: bfloat16 [4096, 2560], P(('groups', 'ctx')), parts along dimension 0, may hold values from -6.2 to 6.2
- value_rows: bfloat16 [4096, 2560], P(('groups', 'ctx')), parts along dimension 0, may hold values from -6 to 6
- out_grad: bfloat16 [4096, 2560], P(('groups', 'ctx')), parts along dimension 0, may hold values from -6 to 6
- selected: int32 [32, 8], P('groups'), parts along dimension 0, may hold values from 0 to 15, as said below
Outputs:
- attended: bfloat16 [4096, 2560], P(('groups', 'ctx')), parts along dimension 0
- grad_query: bfloat16 [4096, 2560], P(('groups', 'ctx')), parts along dimension 0
- grad_key: bfloat16 [4096, 2560], P(('groups', 'ctx')), parts along dimension 0
- grad_value: bfloat16 [4096, 2560], P(('groups', 'ctx')), parts along dimension 0
- pooled_key_grad: float32 [64, 2560], P(('groups', 'ctx')), parts along dimension 0
- pooled_value_grad: float32 [64, 2560], P(('groups', 'ctx')), parts along dimension 0
There are 2 independent parts, one for each index of `groups`. A program takes and returns all parts, laid end to end along the dimension named above; each array names one. Nothing has to cross between parts.
Inputs may be any that keep to these rules, and one draw needn't show every extreme that they name: `selected`: each row names 8 different tiles.
All inputs are finite; a program needn't handle non-finite values.
Results may differ from a plain program's by a relative error of at most 0.029.
Values may be sent and summed in bfloat16 or wider, within the bound.
No kernel may reach another device: no remote copies, remote signals or barrier semaphores. Data moves between devices by JAX's collectives and lax.ppermute only.
A program may use at most 192 MiB of HBM per device.

v0:
```python
import functools

import jax
import jax.numpy as jnp
from jax import lax
from jax.experimental import pallas as pl
from jax.experimental.pallas import tpu as pltpu
from jax.sharding import PartitionSpec as P


HEADS = 20
HEAD_DIM = 128
TILE = 128
POOL = 64
SEL = 8


def pooled(rows):
    return jnp.mean(rows.astype(jnp.float32).reshape(-1, POOL, rows.shape[1]), axis=1).astype(
        jnp.bfloat16
    )


def contract(left, right, left_dim, right_dim):
    return lax.dot_general(
        left, right, (((left_dim,), (right_dim,)), ((), ())), preferred_element_type=jnp.float32
    )


def attend(queries, grads_out, keys_all, values_all):
    scaling = HEAD_DIM ** (-0.5)
    out_parts, query_parts, key_parts, value_parts = ([], [], [], [])
    for head in range(HEADS):
        lower = head * HEAD_DIM
        upper = lower + HEAD_DIM
        head_query = queries[:, lower:upper]
        head_grad = grads_out[:, lower:upper]
        head_key = keys_all[:, lower:upper]
        head_value = values_all[:, lower:upper]
        scores = contract(head_query, head_key, 1, 1) * scaling
        summit = jnp.max(scores, axis=-1, keepdims=True)
        raised = jnp.exp(scores - summit)
        weights = raised / jnp.sum(raised, axis=-1, keepdims=True)
        rounded = weights.astype(jnp.bfloat16)
        out_rows = jnp.dot(rounded, head_value, preferred_element_type=jnp.float32).astype(
            jnp.bfloat16
        )
        row_dots = jnp.sum(
            head_grad.astype(jnp.float32) * out_rows.astype(jnp.float32), axis=-1, keepdims=True
        )
        prob_grad = contract(head_grad, head_value, 1, 1)
        score_grad = (weights * (prob_grad - row_dots)).astype(jnp.bfloat16)
        query_grad = jnp.dot(score_grad, head_key, preferred_element_type=jnp.float32) * scaling
        key_terms = contract(score_grad, head_query, 0, 0) * scaling
        value_terms = contract(rounded, head_grad, 0, 0)
        out_parts.append(out_rows)
        query_parts.append(query_grad.astype(jnp.bfloat16))
        key_parts.append(key_terms)
        value_parts.append(value_terms)
    return (
        jnp.concatenate(out_parts, axis=1),
        jnp.concatenate(query_parts, axis=1),
        jnp.concatenate(key_parts, axis=1),
        jnp.concatenate(value_parts, axis=1),
    )


def package(tiles_in, pooled_in, devices, spread):
    tiles_here, tile_len, columns = tiles_in.shape
    per_tile = tile_len // POOL
    split_rows = tiles_in.reshape(tiles_here, devices, spread, columns)
    copies = jnp.broadcast_to(
        pooled_in.reshape(tiles_here, 1, per_tile, columns),
        (tiles_here, devices, per_tile, columns),
    )
    return jnp.concatenate([split_rows, copies], axis=2).reshape(
        tiles_here, devices * (spread + per_tile), columns
    )


def listed_shards(query_rows, key_rows, value_rows, out_grad, selected):
    height, columns = query_rows.shape
    devices = lax.axis_size("ctx")
    tiles_here = height // TILE
    spread = TILE // devices
    own_keys = pooled(key_rows)
    own_values = pooled(value_rows)
    key_tiles = key_rows.reshape(tiles_here, TILE, columns)
    value_tiles = value_rows.reshape(tiles_here, TILE, columns)
    joined_keys, joined_values = (
        lax.all_to_all(
            package(key_tiles, own_keys, devices, spread),
            "ctx",
            split_axis=1,
            concat_axis=0,
            tiled=True,
        ),
        lax.all_to_all(
            package(value_tiles, own_values, devices, spread),
            "ctx",
            split_axis=1,
            concat_axis=0,
            tiled=True,
        ),
    )
    held_keys = joined_keys[:, :spread]
    held_values = joined_values[:, :spread]
    pool_keys = joined_keys[:, spread:].reshape(-1, columns)
    pool_values = joined_values[:, spread:].reshape(-1, columns)
    comp_count = pool_keys.shape[0]
    got_keys, got_values = (
        lax.all_to_all(held_keys[selected], "ctx", split_axis=0, concat_axis=2, tiled=True),
        lax.all_to_all(held_values[selected], "ctx", split_axis=0, concat_axis=2, tiled=True),
    )
    fine_keys = got_keys.reshape(tiles_here, SEL * TILE, columns)
    fine_values = got_values.reshape(tiles_here, SEL * TILE, columns)
    out_tiles, query_tiles, key_listed, value_listed = ([], [], [], [])
    keys_all = jnp.concatenate([pool_keys, fine_keys[0]], axis=0)
    values_all = jnp.concatenate([pool_values, fine_values[0]], axis=0)
    out_rows, query_grad, key_terms, value_terms = attend(
        query_rows, out_grad, keys_all, values_all
    )
    out_tiles.append(out_rows)
    query_tiles.append(query_grad)
    coarse_keys = key_terms[:comp_count]
    coarse_values = value_terms[:comp_count]
    key_listed.append(key_terms[comp_count:].astype(jnp.bfloat16))
    value_listed.append(value_terms[comp_count:].astype(jnp.bfloat16))
    own_coarse_keys, own_coarse_values = (
        lax.psum_scatter(coarse_keys, "ctx", scatter_dimension=0, tiled=True),
        lax.psum_scatter(coarse_values, "ctx", scatter_dimension=0, tiled=True),
    )
    listed_keys = jnp.stack(key_listed).reshape(tiles_here * SEL, devices, spread, columns)
    listed_values = jnp.stack(value_listed).reshape(tiles_here * SEL, devices, spread, columns)
    back_keys, back_values = (
        lax.all_to_all(listed_keys, "ctx", split_axis=1, concat_axis=0, tiled=True),
        lax.all_to_all(listed_values, "ctx", split_axis=1, concat_axis=0, tiled=True),
    )
    tile_ids = jnp.arange(selected.shape[0], dtype=jnp.int32)[:, None]
    member = (selected.reshape(1, -1) == tile_ids).astype(jnp.bfloat16)
    entries = member.shape[1]
    sum_keys = jnp.dot(
        member, back_keys.reshape(entries, spread * columns), preferred_element_type=jnp.float32
    )
    sum_values = jnp.dot(
        member, back_values.reshape(entries, spread * columns), preferred_element_type=jnp.float32
    )
    held_key_grad = sum_keys.astype(jnp.bfloat16).reshape(devices, tiles_here, spread, columns)
    held_value_grad = sum_values.astype(jnp.bfloat16).reshape(devices, tiles_here, spread, columns)
    owned_keys, owned_values = (
        lax.all_to_all(held_key_grad, "ctx", split_axis=0, concat_axis=2, tiled=True),
        lax.all_to_all(held_value_grad, "ctx", split_axis=0, concat_axis=2, tiled=True),
    )
    grad_key = (
        owned_keys.reshape(height, columns).astype(jnp.float32)
        + jnp.repeat(own_coarse_keys, POOL, axis=0) / POOL
    ).astype(jnp.bfloat16)
    grad_value = (
        owned_values.reshape(height, columns).astype(jnp.float32)
        + jnp.repeat(own_coarse_values, POOL, axis=0) / POOL
    ).astype(jnp.bfloat16)
    attended = out_tiles[0]
    grad_query = query_tiles[0]
    return (attended, grad_query, grad_key, grad_value, own_coarse_keys, own_coarse_values)


LANES = 128
JOBS = 4
SPLITS = 2
VMEM = pl.BlockSpec(memory_space=pltpu.VMEM)
SMEM = pl.BlockSpec(memory_space=pltpu.SMEM)
BIG = pltpu.CompilerParams(vmem_limit_bytes=50 * 1024 * 1024)


def nt(left, right):
    return contract(left, right, 1, 1)


def nn(left, right):
    return contract(left, right, 1, 0)


def split_rows(total):
    parts = []
    for _ in range(SPLITS):
        part = total.astype(jnp.bfloat16)
        parts.append(part.astype(jnp.float32))
        total = total - parts[-1]
    return parts


def tail_rows(coarse_key, coarse_value):
    per_tile = TILE // POOL
    parts = split_rows(jnp.concatenate([coarse_key, coarse_value], axis=0))
    used = SPLITS * 2 * per_tile
    if used < tail_height():
        parts.append(jnp.zeros((tail_height() - used, LANES), jnp.float32))
    return jnp.concatenate(parts, axis=0).astype(jnp.bfloat16)


def tail_height():
    used = SPLITS * 2 * (TILE // POOL)
    return -(-used // 8) * 8


def join_tail(tail):
    pair = 2 * (TILE // POOL)
    rows = tail.astype(jnp.float32)
    total = rows[:pair]
    for part in range(1, SPLITS):
        total = total + rows[part * pair : (part + 1) * pair]
    return total


def lane_block(index):
    return pl.ds(pl.multiple_of(index * LANES, LANES), LANES)


def pack_body(first, place_ref, q_ref, k_ref, v_ref, g_ref, *out_refs):
    for step, out_ref in enumerate(out_refs):
        columns = lane_block(first + lax.bitwise_xor(place_ref[0], step))
        for index, ref in enumerate((q_ref, k_ref, v_ref, g_ref)):
            out_ref[index * TILE : (index + 1) * TILE, :] = ref[:, columns]


def pack(arrays, place, first, count):
    width = arrays[0].shape[1]
    if first % count == 0:
        spec = pl.BlockSpec((TILE, count * LANES), lambda i, _: (0, first // count))
        start = 0
    else:
        spec = pl.BlockSpec((TILE, width), lambda i, _: (0, 0))
        start = first
    out = pl.BlockSpec((4 * TILE, LANES), lambda i, _: (0, 0))
    return pl.pallas_call(
        functools.partial(pack_body, start),
        grid_spec=pltpu.PrefetchScalarGridSpec(
            num_scalar_prefetch=1, grid=(1,), in_specs=[spec] * 4, out_specs=[out] * count
        ),
        out_shape=[jax.ShapeDtypeStruct((4 * TILE, LANES), jnp.bfloat16)] * count,
        cost_estimate=pl.CostEstimate(
            flops=0, transcendentals=0, bytes_accessed=16 * count * TILE * LANES
        ),
        name="pack",
    )(place, *arrays)


def prepare(scratch):
    rows_ref, pool_key, pool_value, key_t, value_t, both_sum, pool_key_sum, pool_value_sum = scratch
    per_tile = TILE // POOL

    def one(tile, carry):
        for place, pool_ref, flip_ref in ((0, pool_key, key_t), (1, pool_value, value_t)):
            rows = rows_ref[tile, :, place * LANES : (place + 1) * LANES].astype(jnp.float32)
            means = [
                jnp.mean(rows[part * POOL : (part + 1) * POOL], axis=0, keepdims=True)
                for part in range(per_tile)
            ]
            pool_ref[pl.ds(tile * per_tile, per_tile), :] = jnp.concatenate(means, axis=0)
            flip_ref[tile] = rows.T.astype(jnp.bfloat16)
        both_sum[tile] = jnp.zeros((TILE, 2 * LANES), jnp.float32)
        return carry

    lax.fori_loop(0, rows_ref.shape[0], one, 0)
    pool_key_sum[...] = jnp.zeros_like(pool_key_sum)
    pool_value_sum[...] = jnp.zeros_like(pool_value_sum)


def wide_pair(left, right):
    zeros = jnp.zeros_like(left)
    return jnp.concatenate(
        [jnp.concatenate([left, zeros], axis=1), jnp.concatenate([zeros, right], axis=1)], axis=0
    )


def some_tiles(jobs, scratch, work):
    rows_ref, pool_key, pool_value, key_t, value_t, both_sum, pool_key_sum, pool_value_sum = scratch
    scaling = HEAD_DIM ** (-0.5)
    base2 = scaling * 1.4426950408889634
    comp = pool_key.shape[0]
    coarse_key = pool_key[...].astype(jnp.bfloat16)
    coarse_value = pool_value[...].astype(jnp.bfloat16)
    coarse = jnp.concatenate([coarse_key, coarse_value], axis=1)
    fine = SEL * TILE
    spans = [(slot * TILE, TILE) for slot in range(SEL)] + [(fine, comp)]
    results = []
    for (query, grad, listed), (score_ref, prob_ref, pair_ref) in zip(jobs, work):
        pair = wide_pair(query, grad)
        rows = [rows_ref[tile] for tile in listed]
        both = nt(jnp.concatenate(rows + [coarse], axis=0), pair)
        score_ref[...] = both[:, :LANES]
        prob_ref[...] = both[:, LANES:]
        top = jnp.max(both[:, :LANES], axis=0, keepdims=True)
        results.append((pair, top))
    for index, (_, (score_ref, prob_ref, pair_ref)) in enumerate(zip(jobs, work)):
        pair, top = results[index]
        raised = jnp.exp2((score_ref[...] - top) * base2)
        score_ref[...] = raised
        inverse = 1.0 / jnp.sum(raised, axis=0, keepdims=True)
        results[index] = (pair, inverse)
    outs = []
    for index, ((query, grad, listed), (score_ref, prob_ref, pair_ref)) in enumerate(zip(jobs, work)):
        pair, inverse = results[index]
        weight = score_ref[...] * inverse
        rounded = weight.astype(jnp.bfloat16)
        pair_ref[:, LANES:] = rounded
        score_ref[...] = weight
        values_t = jnp.concatenate([value_t[tile] for tile in listed], axis=1)
        out_t = nn(values_t, pair_ref[:fine, LANES:]) + contract(
            coarse_value, pair_ref[fine:, LANES:], 0, 0
        )
        out_t = out_t.astype(jnp.bfloat16).astype(jnp.float32)
        dots = jnp.sum(out_t * grad.astype(jnp.float32).T, axis=0, keepdims=True)
        outs.append((out_t, dots))
    for index, ((query, grad, listed), (score_ref, prob_ref, pair_ref)) in enumerate(zip(jobs, work)):
        out_t, dots = outs[index]
        slope = (score_ref[...] * (prob_ref[...] - dots)).astype(jnp.bfloat16)
        pair_ref[:, :LANES] = slope
        terms = nn(pair_ref[...], results[index][0])
        for tile, (start, size) in zip(listed, spans):
            both_sum[tile] += terms[start : start + size]
        pool_key_sum[...] += terms[fine:, :LANES]
        pool_value_sum[...] += terms[fine:, LANES:]
        keys_t = jnp.concatenate([key_t[tile] for tile in listed], axis=1)
        query_t = nn(keys_t, pair_ref[:fine, :LANES]) + contract(
            coarse_key, pair_ref[fine:, :LANES], 0, 0
        )
        outs[index] = (
            out_t.T.astype(jnp.bfloat16),
            (query_t.T * scaling).astype(jnp.bfloat16),
        )
    return outs


def finish(tile, scratch):
    scaling = HEAD_DIM ** (-0.5)
    both_sum, pool_key_sum, pool_value_sum = scratch
    per_tile = TILE // POOL
    coarse_key = pool_key_sum[pl.ds(tile * per_tile, per_tile), :] * scaling
    coarse_value = pool_value_sum[pl.ds(tile * per_tile, per_tile), :]

    def whole(fine, coarse):
        return jnp.concatenate(
            [
                fine[part * POOL : (part + 1) * POOL] + coarse[part : part + 1] * (1.0 / POOL)
                for part in range(per_tile)
            ],
            axis=0,
        )

    return (
        whole(both_sum[tile, :, :LANES] * scaling, coarse_key),
        whole(both_sum[tile, :, LANES:], coarse_value),
        coarse_key,
        coarse_value,
    )


def head_scratch(tiles):
    comp = tiles * (TILE // POOL)
    keys = SEL * TILE + comp
    return [
        pltpu.VMEM((tiles, TILE, 2 * LANES), jnp.bfloat16),
        pltpu.VMEM((comp, LANES), jnp.float32),
        pltpu.VMEM((comp, LANES), jnp.float32),
        pltpu.VMEM((tiles, LANES, TILE), jnp.bfloat16),
        pltpu.VMEM((tiles, LANES, TILE), jnp.bfloat16),
        pltpu.VMEM((tiles, TILE, 2 * LANES), jnp.float32),
        pltpu.VMEM((comp, LANES), jnp.float32),
        pltpu.VMEM((comp, LANES), jnp.float32),
    ] + JOBS * [
        pltpu.VMEM((keys, LANES), jnp.float32),
        pltpu.VMEM((keys, LANES), jnp.float32),
        pltpu.VMEM((keys, 2 * LANES), jnp.bfloat16),
    ]


def split_scratch(scratch):
    totals, work = scratch[:8], scratch[8:]
    return totals, [work[3 * job : 3 * job + 3] for job in range(JOBS)]


def head_cost(queries, keys, moved):
    return pl.CostEstimate(
        flops=12 * queries * keys * LANES,
        transcendentals=queries * keys,
        bytes_accessed=moved,
    )


def every_tile(count, stride, place_ref, sel_ref, query_ref, out_ref, totals, work):
    place = place_ref[0]

    def some(first, carry):
        jobs = []
        for job in range(JOBS):
            piece = first * JOBS + job
            tile = lax.bitwise_xor(place, piece * stride)
            listed = [lax.bitwise_xor(sel_ref[tile, slot], place) for slot in range(SEL)]
            jobs.append((query_ref[piece, :, :LANES], query_ref[piece, :, LANES:], listed))
        for job, (rows, slopes) in enumerate(some_tiles(jobs, totals, work)):
            out_ref[first * JOBS + job, :TILE, :] = rows
            out_ref[first * JOBS + job, TILE : 2 * TILE, :] = slopes
        return carry

    lax.fori_loop(0, count // JOBS, some, 0)


def whole_head(tiles, place_ref, sel_ref, *refs):
    pieces, outs = refs[:tiles][::-1], refs[tiles : 2 * tiles]
    query_ref, out_ref = refs[2 * tiles : 2 * tiles + 2]
    totals, work = split_scratch(refs[2 * tiles + 2 :])
    for step, piece in enumerate(pieces):
        query_ref[step, :, :LANES] = piece[:TILE, :]
        totals[0][step, :, :LANES] = piece[TILE : 2 * TILE, :]
        totals[0][step, :, LANES:] = piece[2 * TILE : 3 * TILE, :]
        query_ref[step, :, LANES:] = piece[3 * TILE :, :]
    prepare(totals)
    every_tile(tiles, 1, place_ref, sel_ref, query_ref, out_ref, totals, work)
    for step, out in enumerate(outs):
        key, value, coarse_key, coarse_value = finish(step, totals[5:])
        out[: 2 * TILE, :] = out_ref[step]
        out[2 * TILE : 3 * TILE, :] = key.astype(jnp.bfloat16)
        out[3 * TILE : 4 * TILE, :] = value.astype(jnp.bfloat16)
        out[4 * TILE :, :] = tail_rows(coarse_key, coarse_value)


def shared_head(span, planes, place_ref, sel_ref, *refs):
    owns, refs = refs[:planes], refs[planes:]
    pieces, refs = refs[: span - 1], refs[span - 1 :]
    out_ref, keep_ref, send_ref, query_ref = refs[:4]
    totals, work = split_scratch(refs[4:])
    for plane, own in enumerate(owns):
        query_ref[plane, :, :LANES] = own[:TILE, :]
        query_ref[plane, :, LANES:] = own[3 * TILE :, :]
        totals[0][plane * span, :, :LANES] = own[TILE : 2 * TILE, :]
        totals[0][plane * span, :, LANES:] = own[2 * TILE : 3 * TILE, :]
        for step in range(1, span):
            piece = pieces[step - 1]
            totals[0][plane * span + step, :, :LANES] = piece[plane, :TILE, :]
            totals[0][plane * span + step, :, LANES:] = piece[plane, TILE:, :]
    prepare(totals)
    every_tile(planes, span, place_ref, sel_ref, query_ref, out_ref, totals, work)
    for step in range(span):

        def last(plane, carry, step=step):
            terms = finish(plane * span + step, totals[5:])
            if step % 2 == 0:
                keep_terms(keep_ref, step // 2, plane, *terms)
            else:
                send_terms(send_ref, step // 2, plane, *terms)
            return carry

        lax.fori_loop(0, planes, last, 0)


def keep_terms(ref, index, plane, key, value, coarse_key, coarse_value):
    rows = [coarse_key, coarse_value]
    filler = 8 - 2 * (TILE // POOL)
    if filler:
        rows.append(jnp.zeros((filler, LANES), jnp.float32))
    ref[index, plane, :TILE, :] = key
    ref[index, plane, TILE : 2 * TILE, :] = value
    ref[index, plane, 2 * TILE :, :] = jnp.concatenate(rows, axis=0)


def send_terms(ref, index, plane, key, value, coarse_key, coarse_value):
    ref[index, plane, :TILE, :] = key.astype(jnp.bfloat16)
    ref[index, plane, TILE : 2 * TILE, :] = value.astype(jnp.bfloat16)
    ref[index, plane, 2 * TILE :, :] = tail_rows(coarse_key, coarse_value)


def add_terms(keep_ref, piece_ref, index, plane):
    per_tile = TILE // POOL
    fine = keep_ref[index, plane, : 2 * TILE, :]
    fine = fine + piece_ref[index, plane, : 2 * TILE, :].astype(jnp.float32)
    coarse = keep_ref[index, plane, 2 * TILE : 2 * TILE + 2 * per_tile, :]
    coarse = coarse + join_tail(piece_ref[index, plane, 2 * TILE :, :])
    return fine[:TILE], fine[TILE:], coarse[:per_tile], coarse[per_tile:]


def fold_terms(count, planes, keep_ref, piece_ref, next_ref, send_ref):
    for index in range(count):
        for plane in range(planes):
            terms = add_terms(keep_ref, piece_ref, index, plane)
            if index % 2 == 0:
                keep_terms(next_ref, index // 2, plane, *terms)
            else:
                send_terms(send_ref, index // 2, plane, *terms)


def last_terms(rows_ref, keep_ref, piece_ref, *outs):
    for plane, out in enumerate(outs):
        key, value, coarse_key, coarse_value = add_terms(keep_ref, piece_ref, 0, plane)
        out[: 2 * TILE, :] = rows_ref[plane]
        out[2 * TILE : 3 * TILE, :] = key.astype(jnp.bfloat16)
        out[3 * TILE : 4 * TILE, :] = value.astype(jnp.bfloat16)
        out[4 * TILE :, :] = tail_rows(coarse_key, coarse_value)


def unpack_body(heads, span, place_ref, *refs):
    pieces, (a_ref, q_ref, k_ref, v_ref, pk_ref, pv_ref) = refs[:-6], refs[-6:]
    pieces = pieces[:heads][::-1] + pieces[heads:][::-1]
    per_tile = TILE // POOL
    place = place_ref[0]
    for step, ref in enumerate(pieces):
        if step < heads:
            head = lax.bitwise_xor(place, step)
        else:
            head = heads + lax.bitwise_xor(place // span, step - heads)
        columns = lane_block(head)
        for index, out in enumerate((a_ref, q_ref, k_ref, v_ref)):
            out[:, columns] = ref[index * TILE : (index + 1) * TILE, :]
        coarse = join_tail(ref[4 * TILE :, :])
        pk_ref[:, columns] = coarse[:per_tile]
        pv_ref[:, columns] = coarse[per_tile:]


def head_shards(query_rows, key_rows, value_rows, out_grad, selected):
    devices = lax.axis_size("ctx")
    height, columns = query_rows.shape
    planes = HEADS - devices
    span = devices // planes
    arrays = (query_rows, key_rows, value_rows, out_grad)
    place = jnp.reshape(lax.axis_index("ctx"), (1,))

    def shift(block, step):
        return lax.ppermute(block, "ctx", [(i, i ^ step) for i in range(devices)])

    def spread(pieces, stride):
        moved = [pieces[0]]
        for step in range(1, len(pieces)):
            moved.append(shift(pieces[step], step * stride))
        return moved

    def shape(*dims, dtype=jnp.bfloat16):
        return jax.ShapeDtypeStruct(dims, dtype)

    block = 4 * TILE + tail_height()
    part = 2 * TILE + tail_height()
    keys = SEL * TILE + devices * (TILE // POOL)
    owns = spread(pack(arrays, place // span, devices, planes), span)
    mains = spread(pack(arrays, place, 0, devices), 1)
    own_kv = jnp.stack([own[TILE : 3 * TILE] for own in owns])
    pieces = {0: own_kv}
    hops = [1 << bit for bit in reversed(range(span.bit_length() - 1))]
    for hop in hops:
        held = sorted(pieces)
        for step in held:
            pieces[step ^ hop] = shift(pieces[step], hop)
    pieces = [pieces[step] for step in range(1, span)]
    half = span // 2
    rows, keep, send = pl.pallas_call(
        functools.partial(shared_head, span, planes),
        in_specs=[SMEM, SMEM] + [VMEM] * (planes + span - 1),
        out_specs=[VMEM] * 3,
        out_shape=[
            shape(planes, 2 * TILE, LANES),
            shape(half, planes, 2 * TILE + 8, LANES, dtype=jnp.float32),
            shape(half, planes, part, LANES),
        ],
        scratch_shapes=[pltpu.VMEM((planes, TILE, 2 * LANES), jnp.bfloat16)]
        + head_scratch(devices),
        compiler_params=BIG,
        cost_estimate=head_cost(planes * TILE, keys, 16 * devices * TILE * LANES),
        name="shared_head",
    )(place, selected, *owns, *pieces)
    hop = 1
    while half > 1:
        got = shift(send, hop)
        keep, send = pl.pallas_call(
            functools.partial(fold_terms, half, planes),
            in_specs=[VMEM] * 2,
            out_specs=[VMEM] * 2,
            out_shape=[
                shape(half // 2, planes, 2 * TILE + 8, LANES, dtype=jnp.float32),
                shape(half // 2, planes, part, LANES),
            ],
            compiler_params=BIG,
            name="fold_terms",
        )(keep, got)
        half, hop = half // 2, hop * 2
    got = shift(send, hop)
    rests = pl.pallas_call(
        last_terms,
        in_specs=[VMEM] * 3,
        out_specs=[VMEM] * planes,
        out_shape=[shape(block, LANES)] * planes,
        compiler_params=BIG,
        name="last_terms",
    )(rows, keep, got)
    rests = spread(rests, span)
    dones = pl.pallas_call(
        functools.partial(whole_head, devices),
        in_specs=[SMEM, SMEM] + [VMEM] * devices,
        out_specs=[VMEM] * devices,
        out_shape=[shape(block, LANES)] * devices,
        scratch_shapes=[
            pltpu.VMEM((devices, TILE, 2 * LANES), jnp.bfloat16),
            pltpu.VMEM((devices, 2 * TILE, LANES), jnp.bfloat16),
        ]
        + head_scratch(devices),
        compiler_params=BIG,
        cost_estimate=head_cost(devices * TILE, keys, 16 * devices * TILE * LANES),
        name="whole_head",
    )(place, selected, *mains[::-1])
    dones = spread(dones, 1)
    wide = shape(height, columns)
    thin = shape(height // POOL, columns, dtype=jnp.float32)
    return pl.pallas_call(
        functools.partial(unpack_body, devices, span),
        in_specs=[SMEM] + [VMEM] * HEADS,
        out_specs=[VMEM] * 6,
        out_shape=[wide, wide, wide, wide, thin, thin],
        compiler_params=BIG,
        name="unpack",
    )(place, *dones[::-1], *rests[::-1])


def shards(query_rows, key_rows, value_rows, out_grad, selected):
    devices = lax.axis_size("ctx")
    planes = HEADS - devices
    tiles_here = query_rows.shape[0] // TILE
    if planes > 0 and devices % planes == 0 and tiles_here == 1 and planes % JOBS == 0:
        span = devices // planes
        if span & (span - 1) == 0:
            return head_shards(query_rows, key_rows, value_rows, out_grad, selected)
    return listed_shards(query_rows, key_rows, value_rows, out_grad, selected)


def solution(mesh):
    in_specs = (
        P(("groups", "ctx"), None),
        P(("groups", "ctx"), None),
        P(("groups", "ctx"), None),
        P(("groups", "ctx"), None),
        P("groups", None),
    )
    out_specs = (
        P(("groups", "ctx"), None),
        P(("groups", "ctx"), None),
        P(("groups", "ctx"), None),
        P(("groups", "ctx"), None),
        P(("groups", "ctx"), None),
        P(("groups", "ctx"), None),
    )
    return jax.shard_map(
        shards, mesh=mesh, in_specs=in_specs, out_specs=out_specs, check_vma=False
    )
```

profile of v0, /device:TPU:1, one launch (start us, length us, event | category | flops | bytes accessed | tf_op | source)
XLA Modules:
  0.0 188.0 jit_solution(3566578996613582312)
XLA Ops:
  0.7 2.0 %pack.3 = (bf16[512,128]{1,0:T(8,128)(2,1)}, bf16[512,128]{1,0:T(8,128)(2,1)}, bf16[512,128]{1,0:T(8,128)(2,1)}, bf16[512,128]{1,0:T(8,128)(2,1)}) custom-call(s32[1]{0:T(128)S(6)} %select_n.5.place_ref, bf16[128,2560]{1,0:T(8,128)(2,1)} %q_ref.3, bf16[128,2560]{1,0:T(8,128)(2,1)} %k_ref.3, bf16[128,2560]{1,0:T(8,128)(2,1)} %v_ref.3, bf16[128,2560]{1,0:T(8,128)(2,1)} %g_ref.3), custom_call_target="tpu_custom_call" | custom-call | bytes 1048576 | tf_op jit(solution)/shard_map/pack/pallas_call | solution.py:235
  2.6 2.1 %collective-permute-start.30 = (bf16[512,128]{1,0:T(8,128)(2,1)}, bf16[512,128]{1,0:T(8,128)(2,1)S(1)}, u32[]{:S(2)}, u32[]{:S(2)}) collective-permute-start(bf16[512,128]{1,0:T(8,128)(2,1)} %get-tuple-element.84), channel_id=1, source_target_pairs={{0,4},{1,5},{2,6},{3,7},{4,0},{5,1},{6,2},{7,3},{8,12},{9,13},{10,... | collective-permute-start | bytes 393224 | tf_op jit(solution)/shard_map/ppermute | solution.py:528
  4.8 2.3 %collective-permute-start.31 = (bf16[512,128]{1,0:T(8,128)(2,1)}, bf16[512,128]{1,0:T(8,128)(2,1)S(1)}, u32[]{:S(2)}, u32[]{:S(2)}) collective-permute-start(bf16[512,128]{1,0:T(8,128)(2,1)} %get-tuple-element.85), channel_id=1, source_target_pairs={{0,8},{1,9},{2,10},{3,11},{4,12},{5,13},{6,14},{7,15},{8,0},{9,1},... | collective-permute-start | bytes 393224 | tf_op jit(solution)/shard_map/ppermute | solution.py:528
  8.2 2.2 %collective-permute-done.31.refs_2_ = bf16[512,128]{1,0:T(8,128)(2,1)S(1)} collective-permute-done((bf16[512,128]{1,0:T(8,128)(2,1)}, bf16[512,128]{1,0:T(8,128)(2,1)S(1)}, u32[]{:S(2)}, u32[]{:S(2)}) %collective-permute-start.31) | collective-permute-done | bytes 131104 | tf_op jit(solution)/shard_map/ppermute | solution.py:528
  10.3 5.4 %collective-permute-done.32.refs_3_ = bf16[512,128]{1,0:T(8,128)(2,1)S(1)} collective-permute-done((bf16[512,128]{1,0:T(8,128)(2,1)}, bf16[512,128]{1,0:T(8,128)(2,1)S(1)}, u32[]{:S(2)}, u32[]{:S(2)}) %collective-permute-start.32) | collective-permute-done | bytes 131104 | tf_op jit(solution)/shard_map/ppermute | solution.py:528
  15.8 1.3 collective-permute-start.34
  17.1 3.4 %collective-permute-start.33 = (bf16[4,256,128]{2,1,0:T(8,128)(2,1)S(1)}, bf16[4,256,128]{2,1,0:T(8,128)(2,1)S(1)}, u32[]{:S(2)}, u32[]{:S(2)}) collective-permute-start(bf16[4,256,128]{2,1,0:T(8,128)(2,1)S(1)} %pad_maximum_fusion), channel_id=1, source_target_pairs={{0,1},{1,0},{2,3},{3,2},{4,5},{5,4},{6,7},{7,6},{8,9},{9,8},{10,11... | collective-permute-start | bytes 786440 | tf_op jit(solution)/shard_map/ppermute | solution.py:528
  21.1 4.2 %collective-permute-start.35 = (bf16[4,256,128]{2,1,0:T(8,128)(2,1)S(1)}, bf16[4,256,128]{2,1,0:T(8,128)(2,1)S(1)}, u32[]{:S(2)}, u32[]{:S(2)}) collective-permute-start(bf16[4,256,128]{2,1,0:T(8,128)(2,1)S(1)} %collective-permute-done.34.refs_5_), channel_id=1, source_target_pairs={{0,1},{1,0},{2,3},{3,2},{4,5},{5,4},{6,7},{7,6},{8,9},{9,8},{10,11... | collective-permute-start | bytes 786440 | tf_op jit(solution)/shard_map/ppermute | solution.py:528
  27.4 6.1 %shared_head.1 = (bf16[4,256,128]{2,1,0:T(8,128)(2,1)S(1)}, f32[2,4,264,128]{3,2,1,0:T(8,128)S(1)}, bf16[2,4,264,128]{3,2,1,0:T(8,128)(2,1)S(1)}) custom-call(s32[1]{0:T(128)} %bitcast.place_ref, s32[16,8]{1,0:T(8,128)S(1)} %copy.11.sel_ref, bf16[512,128]{1,0:T(8,128)(2,1)S(1)} %copy-done, bf16[512,128]{1,0:T(8,128)(2,1)S(1)} %collective-permute-done.30.refs_1_, ...), custom_call_target="tpu_custom_call" | custom-call | flops 830472192 | bytes 4194304 | tf_op jit(solution)/shard_map/shared_head/pallas_call | solution.py:553
  33.9 3.4 %pack.2 = (bf16[512,128]{1,0:T(8,128)(2,1)}, bf16[512,128]{1,0:T(8,128)(2,1)}, bf16[512,128]{1,0:T(8,128)(2,1)}, bf16[512,128]{1,0:T(8,128)(2,1)}, bf16[512,128]...) custom-call(s32[1]{0:T(128)} %bitcast.place_ref, ...), custom_call_target="tpu_custom_call" | custom-call | bytes 4194304 | tf_op jit(solution)/shard_map/pack/pallas_call | solution.py:235
  37.3 3.0 %collective-permute-start = (bf16[512,128]{1,0:T(8,128)(2,1)}, bf16[512,128]{1,0:T(8,128)(2,1)S(1)}, u32[]{:S(2)}, u32[]{:S(2)}) collective-permute-start(bf16[512,128]{1,0:T(8,128)(2,1)} %get-tuple-element.51), channel_id=1, source_target_pairs={{0,15},{1,14},{2,13},{3,12},{4,11},{5,10},{6,9},{7,8},{8,7},{9,6},... | collective-permute-start | bytes 393224 | tf_op jit(solution)/shard_map/ppermute | solution.py:528
  40.3 1.2 collective-permute-start.1
  41.5 2.5 %collective-permute-start.2 = (bf16[512,128]{1,0:T(8,128)(2,1)}, bf16[512,128]{1,0:T(8,128)(2,1)S(1)}, u32[]{:S(2)}, u32[]{:S(2)}) collective-permute-start(bf16[512,128]{1,0:T(8,128)(2,1)} %get-tuple-element.53), channel_id=1, source_target_pairs={{0,13},{1,12},{2,15},{3,14},{4,9},{5,8},{6,11},{7,10},{8,5},{9,4},... | collective-permute-start | bytes 393224 | tf_op jit(solution)/shard_map/ppermute | solution.py:528
  44.1 1.3 collective-permute-start.3
  45.6 13.7 %collective-permute-start.4 = (bf16[512,128]{1,0:T(8,128)(2,1)}, bf16[512,128]{1,0:T(8,128)(2,1)S(1)}, u32[]{:S(2)}, u32[]{:S(2)}) collective-permute-start(bf16[512,128]{1,0:T(8,128)(2,1)} %get-tuple-element.55), channel_id=1, source_target_pairs={{0,11},{1,10},{2,9},{3,8},{4,15},{5,14},{6,13},{7,12},{8,3},{9,2},... | collective-permute-start | bytes 393224 | tf_op jit(solution)/shard_map/ppermute | solution.py:528
  59.3 2.5 %collective-permute-start.5 = (bf16[512,128]{1,0:T(8,128)(2,1)}, bf16[512,128]{1,0:T(8,128)(2,1)S(1)}, u32[]{:S(2)}, u32[]{:S(2)}) collective-permute-start(bf16[512,128]{1,0:T(8,128)(2,1)} %get-tuple-element.56), channel_id=1, source_target_pairs={{0,10},{1,11},{2,8},{3,9},{4,14},{5,15},{6,12},{7,13},{8,2},{9,3},... | collective-permute-start | bytes 393224 | tf_op jit(solution)/shard_map/ppermute | solution.py:528
  61.8 7.8 %collective-permute-start.6 = (bf16[512,128]{1,0:T(8,128)(2,1)}, bf16[512,128]{1,0:T(8,128)(2,1)S(1)}, u32[]{:S(2)}, u32[]{:S(2)}) collective-permute-start(bf16[512,128]{1,0:T(8,128)(2,1)} %get-tuple-element.57), channel_id=1, source_target_pairs={{0,9},{1,8},{2,11},{3,10},{4,13},{5,12},{6,15},{7,14},{8,1},{9,0},... | collective-permute-start | bytes 393224 | tf_op jit(solution)/shard_map/ppermute | solution.py:528
  69.6 2.5 %collective-permute-start.7 = (bf16[512,128]{1,0:T(8,128)(2,1)}, bf16[512,128]{1,0:T(8,128)(2,1)S(1)}, u32[]{:S(2)}, u32[]{:S(2)}) collective-permute-start(bf16[512,128]{1,0:T(8,128)(2,1)} %get-tuple-element.58), channel_id=1, source_target_pairs={{0,8},{1,9},{2,10},{3,11},{4,12},{5,13},{6,14},{7,15},{8,0},{9,1},... | collective-permute-start | bytes 393224 | tf_op jit(solution)/shard_map/ppermute | solution.py:528
  72.1 7.3 %collective-permute-done.4.refs_4_ = bf16[512,128]{1,0:T(8,128)(2,1)S(1)} collective-permute-done((bf16[512,128]{1,0:T(8,128)(2,1)}, bf16[512,128]{1,0:T(8,128)(2,1)S(1)}, u32[]{:S(2)}, u32[]{:S(2)}) %collective-permute-start.4) | collective-permute-done | bytes 131104 | tf_op jit(solution)/shard_map/ppermute | solution.py:528
  79.5 2.8 %collective-permute-done.5.refs_5_ = bf16[512,128]{1,0:T(8,128)(2,1)S(1)} collective-permute-done((bf16[512,128]{1,0:T(8,128)(2,1)}, bf16[512,128]{1,0:T(8,128)(2,1)S(1)}, u32[]{:S(2)}, u32[]{:S(2)}) %collective-permute-start.5) | collective-permute-done | bytes 131104 | tf_op jit(solution)/shard_map/ppermute | solution.py:528
  82.3 3.0 %collective-permute-done.6.refs_6_ = bf16[512,128]{1,0:T(8,128)(2,1)S(1)} collective-permute-done((bf16[512,128]{1,0:T(8,128)(2,1)}, bf16[512,128]{1,0:T(8,128)(2,1)S(1)}, u32[]{:S(2)}, u32[]{:S(2)}) %collective-permute-start.6) | collective-permute-done | bytes 131104 | tf_op jit(solution)/shard_map/ppermute | solution.py:528
  85.3 2.6 %collective-permute-done.7.refs_7_ = bf16[512,128]{1,0:T(8,128)(2,1)S(1)} collective-permute-done((bf16[512,128]{1,0:T(8,128)(2,1)}, bf16[512,128]{1,0:T(8,128)(2,1)S(1)}, u32[]{:S(2)}, u32[]{:S(2)}) %collective-permute-start.7) | collective-permute-done | bytes 131104 | tf_op jit(solution)/shard_map/ppermute | solution.py:528
  88.0 2.8 %collective-permute-done.8.refs_8_ = bf16[512,128]{1,0:T(8,128)(2,1)S(1)} collective-permute-done((bf16[512,128]{1,0:T(8,128)(2,1)}, bf16[512,128]{1,0:T(8,128)(2,1)S(1)}, u32[]{:S(2)}, u32[]{:S(2)}) %collective-permute-start.8) | collective-permute-done | bytes 131104 | tf_op jit(solution)/shard_map/ppermute | solution.py:528
  90.7 1.5 collective-permute-start.12
  92.2 1.3 collective-permute-done.9.refs_9_
  93.5 1.2 collective-permute-start.13
  96.7 2.5 %collective-permute-done.11.refs_11_ = bf16[512,128]{1,0:T(8,128)(2,1)S(1)} collective-permute-done((bf16[512,128]{1,0:T(8,128)(2,1)}, bf16[512,128]{1,0:T(8,128)(2,1)S(1)}, u32[]{:S(2)}, u32[]{:S(2)}) %collective-permute-start.11) | collective-permute-done | bytes 131104 | tf_op jit(solution)/shard_map/ppermute | solution.py:528
  99.2 16.5 %whole_head.1 = (bf16[520,128]{1,0:T(8,128)(2,1)S(1)}, bf16[520,128]{1,0:T(8,128)(2,1)S(1)}, bf16[520,128]{1,0:T(8,128)(2,1)S(1)}, bf16[520,128]{1,0:T(8,128)(2,...) custom-call(s32[1]{0:T(128)} %bitcast.place_ref, ...), custom_call_target="tpu_custom_call" | custom-call | flops 3321888768 | bytes 4194304 | tf_op jit(solution)/shard_map/whole_head/pallas_call | solution.py:593
  115.7 4.1 %collective-permute-start.15 = (bf16[520,128]{1,0:T(8,128)(2,1)}, bf16[520,128]{1,0:T(8,128)(2,1)S(1)}, u32[]{:S(2)}, u32[]{:S(2)}) collective-permute-start(bf16[520,128]{1,0:T(8,128)(2,1)} %get-tuple-element.67), channel_id=1, source_target_pairs={{0,15},{1,14},{2,13},{3,12},{4,11},{5,10},{6,9},{7,8},{8,7},{9,6},... | collective-permute-start | bytes 399368 | tf_op jit(solution)/shard_map/ppermute | solution.py:528
  120.8 1.6 collective-permute-start.17
  122.4 1.3 collective-permute-start.18
  124.3 11.0 %collective-permute-start.19 = (bf16[520,128]{1,0:T(8,128)(2,1)S(1)}, bf16[520,128]{1,0:T(8,128)(2,1)S(1)}, u32[]{:S(2)}, u32[]{:S(2)}) collective-permute-start(bf16[520,128]{1,0:T(8,128)(2,1)S(1)} %get-tuple-element.71), channel_id=1, source_target_pairs={{0,11},{1,10},{2,9},{3,8},{4,15},{5,14},{6,13},{7,12},{8,3},{9,2},... | collective-permute-start | bytes 399368 | tf_op jit(solution)/shard_map/ppermute | solution.py:528
  135.4 2.3 %collective-permute-start.20 = (bf16[520,128]{1,0:T(8,128)(2,1)S(1)}, bf16[520,128]{1,0:T(8,128)(2,1)S(1)}, u32[]{:S(2)}, u32[]{:S(2)}) collective-permute-start(bf16[520,128]{1,0:T(8,128)(2,1)S(1)} %get-tuple-element.72), channel_id=1, source_target_pairs={{0,10},{1,11},{2,8},{3,9},{4,14},{5,15},{6,12},{7,13},{8,2},{9,3},... | collective-permute-start | bytes 399368 | tf_op jit(solution)/shard_map/ppermute | solution.py:528
  137.7 8.2 %collective-permute-start.21 = (bf16[520,128]{1,0:T(8,128)(2,1)S(1)}, bf16[520,128]{1,0:T(8,128)(2,1)S(1)}, u32[]{:S(2)}, u32[]{:S(2)}) collective-permute-start(bf16[520,128]{1,0:T(8,128)(2,1)S(1)} %get-tuple-element.73), channel_id=1, source_target_pairs={{0,9},{1,8},{2,11},{3,10},{4,13},{5,12},{6,15},{7,14},{8,1},{9,0},... | collective-permute-start | bytes 399368 | tf_op jit(solution)/shard_map/ppermute | solution.py:528
  145.9 5.1 %collective-permute-start.22 = (bf16[520,128]{1,0:T(8,128)(2,1)S(1)}, bf16[520,128]{1,0:T(8,128)(2,1)S(1)}, u32[]{:S(2)}, u32[]{:S(2)}) collective-permute-start(bf16[520,128]{1,0:T(8,128)(2,1)S(1)} %get-tuple-element.74), channel_id=1, source_target_pairs={{0,8},{1,9},{2,10},{3,11},{4,12},{5,13},{6,14},{7,15},{8,0},{9,1},... | collective-permute-start | bytes 399368 | tf_op jit(solution)/shard_map/ppermute | solution.py:528
  151.0 1.8 collective-permute-done.19.refs_4_
  152.8 6.7 %collective-permute-done.20.refs_5_ = bf16[520,128]{1,0:T(8,128)(2,1)S(1)} collective-permute-done((bf16[520,128]{1,0:T(8,128)(2,1)S(1)}, bf16[520,128]{1,0:T(8,128)(2,1)S(1)}, u32[]{:S(2)}, u32[]{:S(2)}) %collective-permute-start.20) | collective-permute-done | bytes 133152 | tf_op jit(solution)/shard_map/ppermute | solution.py:528
  159.5 2.0 %collective-permute-done.21.refs_6_ = bf16[520,128]{1,0:T(8,128)(2,1)S(1)} collective-permute-done((bf16[520,128]{1,0:T(8,128)(2,1)S(1)}, bf16[520,128]{1,0:T(8,128)(2,1)S(1)}, u32[]{:S(2)}, u32[]{:S(2)}) %collective-permute-start.21) | collective-permute-done | bytes 133152 | tf_op jit(solution)/shard_map/ppermute | solution.py:528
  161.6 2.8 %collective-permute-done.22.refs_7_ = bf16[520,128]{1,0:T(8,128)(2,1)S(1)} collective-permute-done((bf16[520,128]{1,0:T(8,128)(2,1)S(1)}, bf16[520,128]{1,0:T(8,128)(2,1)S(1)}, u32[]{:S(2)}, u32[]{:S(2)}) %collective-permute-start.22) | collective-permute-done | bytes 133152 | tf_op jit(solution)/shard_map/ppermute | solution.py:528
  164.9 2.6 %collective-permute-done.23.refs_8_ = bf16[520,128]{1,0:T(8,128)(2,1)S(1)} collective-permute-done((bf16[520,128]{1,0:T(8,128)(2,1)S(1)}, bf16[520,128]{1,0:T(8,128)(2,1)S(1)}, u32[]{:S(2)}, u32[]{:S(2)}) %collective-permute-start.23) | collective-permute-done | bytes 133152 | tf_op jit(solution)/shard_map/ppermute | solution.py:528
  168.4 2.0 %collective-permute-done.24.refs_9_ = bf16[520,128]{1,0:T(8,128)(2,1)S(1)} collective-permute-done((bf16[520,128]{1,0:T(8,128)(2,1)S(1)}, bf16[520,128]{1,0:T(8,128)(2,1)S(1)}, u32[]{:S(2)}, u32[]{:S(2)}) %collective-permute-start.24) | collective-permute-done | bytes 133152 | tf_op jit(solution)/shard_map/ppermute | solution.py:528
  170.9 2.1 %collective-permute-done.25.refs_10_ = bf16[520,128]{1,0:T(8,128)(2,1)S(1)} collective-permute-done((bf16[520,128]{1,0:T(8,128)(2,1)S(1)}, bf16[520,128]{1,0:T(8,128)(2,1)S(1)}, u32[]{:S(2)}, u32[]{:S(2)}) %collective-permute-start.25) | collective-permute-done | bytes 133152 | tf_op jit(solution)/shard_map/ppermute | solution.py:528
  173.0 1.3 collective-permute-start.38
  174.4 1.5 collective-permute-done.26.refs_11_
  175.9 1.7 collective-permute-start.40
  177.6 2.0 %collective-permute-done.38.refs_16_ = bf16[520,128]{1,0:T(8,128)(2,1)S(1)} collective-permute-done((bf16[520,128]{1,0:T(8,128)(2,1)S(1)}, bf16[520,128]{1,0:T(8,128)(2,1)S(1)}, u32[]{:S(2)}, u32[]{:S(2)}) %collective-permute-start.38) | collective-permute-done | bytes 133152 | tf_op jit(solution)/shard_map/ppermute | solution.py:528
  179.6 6.5 %collective-permute-done.39.refs_17_ = bf16[520,128]{1,0:T(8,128)(2,1)S(1)} collective-permute-done((bf16[520,128]{1,0:T(8,128)(2,1)S(1)}, bf16[520,128]{1,0:T(8,128)(2,1)S(1)}, u32[]{:S(2)}, u32[]{:S(2)}) %collective-permute-start.39) | collective-permute-done | bytes 133152 | tf_op jit(solution)/shard_map/ppermute | solution.py:528
  186.0 2.0 %unpack.1 = (bf16[128,2560]{1,0:T(8,128)(2,1)}, bf16[128,2560]{1,0:T(8,128)(2,1)}, bf16[128,2560]{1,0:T(8,128)(2,1)}, bf16[128,2560]{1,0:T(8,128)(2,1)}, f32[2,2560]{1,0:T(2,128)}, /*index=5*/f32[2,2560]{1,0:T(2,128)}) custom-call(s32[1]{0:T(128)} %bitcast.place_ref, bf16[520,128]{1,0:T(8,128)(2,1)S(1)} %collective-permute-done.15.refs_0_, ...), custom_call_target="tpu_custom_call" | custom-call | tf_op jit(solution)/shard_map/unpack/pallas_call | solution.py:610
  (53 shorter events, 10.3 us)
Async XLA Ops:
  0.6 24.7 %copy-start.2 = (s32[16,8]{0,1:T(8,128)S(1)}, s32[16,8]{0,1:T(8,128)}, u32[]{:S(2)}) copy-start(s32[16,8]{0,1:T(8,128)} %param.9) | copy-start | bytes 1540
  2.6 5.5 %collective-permute-start.30 = (bf16[512,128]{1,0:T(8,128)(2,1)}, bf16[512,128]{1,0:T(8,128)(2,1)S(1)}, u32[]{:S(2)}, u32[]{:S(2)}) collective-permute-start(bf16[512,128]{1,0:T(8,128)(2,1)} %get-tuple-element.84), channel_id=1, source_target_pairs={{0,4},{1,5},{2,6},{3,7},{4,0},{5,1},{6,2},{7,3},{8,12},{9,13},{10,... | collective-permute-start | bytes 393224 | tf_op jit(solution)/shard_map/ppermute | solution.py:528
  4.8 5.6 %collective-permute-start.31 = (bf16[512,128]{1,0:T(8,128)(2,1)}, bf16[512,128]{1,0:T(8,128)(2,1)S(1)}, u32[]{:S(2)}, u32[]{:S(2)}) collective-permute-start(bf16[512,128]{1,0:T(8,128)(2,1)} %get-tuple-element.85), channel_id=1, source_target_pairs={{0,8},{1,9},{2,10},{3,11},{4,12},{5,13},{6,14},{7,15},{8,0},{9,1},... | collective-permute-start | bytes 393224 | tf_op jit(solution)/shard_map/ppermute | solution.py:528
  7.1 8.7 %collective-permute-start.32 = (bf16[512,128]{1,0:T(8,128)(2,1)}, bf16[512,128]{1,0:T(8,128)(2,1)S(1)}, u32[]{:S(2)}, u32[]{:S(2)}) collective-permute-start(bf16[512,128]{1,0:T(8,128)(2,1)} %get-tuple-element.86), channel_id=1, source_target_pairs={{0,12},{1,13},{2,14},{3,15},{4,8},{5,9},{6,10},{7,11},{8,4},{9,5},... | collective-permute-start | bytes 393224 | tf_op jit(solution)/shard_map/ppermute | solution.py:528
  15.8 5.3 %collective-permute-start.34 = (bf16[4,256,128]{2,1,0:T(8,128)(2,1)S(1)}, bf16[4,256,128]{2,1,0:T(8,128)(2,1)S(1)}, u32[]{:S(2)}, u32[]{:S(2)}) collective-permute-start(bf16[4,256,128]{2,1,0:T(8,128)(2,1)S(1)} %pad_maximum_fusion), channel_id=1, source_target_pairs={{0,2},{1,3},{2,0},{3,1},{4,6},{5,7},{6,4},{7,5},{8,10},{9,11},{10,... | collective-permute-start | bytes 786440 | tf_op jit(solution)/shard_map/ppermute | solution.py:528
  17.1 8.3 %collective-permute-start.33 = (bf16[4,256,128]{2,1,0:T(8,128)(2,1)S(1)}, bf16[4,256,128]{2,1,0:T(8,128)(2,1)S(1)}, u32[]{:S(2)}, u32[]{:S(2)}) collective-permute-start(bf16[4,256,128]{2,1,0:T(8,128)(2,1)S(1)} %pad_maximum_fusion), channel_id=1, source_target_pairs={{0,1},{1,0},{2,3},{3,2},{4,5},{5,4},{6,7},{7,6},{8,9},{9,8},{10,11... | collective-permute-start | bytes 786440 | tf_op jit(solution)/shard_map/ppermute | solution.py:528
  21.1 5.4 %collective-permute-start.35 = (bf16[4,256,128]{2,1,0:T(8,128)(2,1)S(1)}, bf16[4,256,128]{2,1,0:T(8,128)(2,1)S(1)}, u32[]{:S(2)}, u32[]{:S(2)}) collective-permute-start(bf16[4,256,128]{2,1,0:T(8,128)(2,1)S(1)} %collective-permute-done.34.refs_5_), channel_id=1, source_target_pairs={{0,1},{1,0},{2,3},{3,2},{4,5},{5,4},{6,7},{7,6},{8,9},{9,8},{10,11... | collective-permute-start | bytes 786440 | tf_op jit(solution)/shard_map/ppermute | solution.py:528
  26.5 0.9 copy-start
  33.5 61.3 %collective-permute-start.36 = (bf16[2,4,264,128]{3,2,1,0:T(8,128)(2,1)S(1)}, bf16[2,4,264,128]{3,2,1,0:T(8,128)(2,1)S(1)}, u32[]{:S(2)}, u32[]{:S(2)}) collective-permute-start(bf16[2,4,264,128]{3,2,1,0:T(8,128)(2,1)S(1)} %get-tuple-element.89), channel_id=1, source_target_pairs={{0,1},{1,0},{2,3},{3,2},{4,5},{5,4},{6,7},{7,6},{8,9},{9,8},{10,11... | collective-permute-start | bytes 1622024 | tf_op jit(solution)/shard_map/ppermute | solution.py:528
  37.3 61.9 %copy-start.1 = (bf16[512,128]{1,0:T(8,128)(2,1)S(1)}, bf16[512,128]{1,0:T(8,128)(2,1)}, u32[]{:S(2)}) copy-start(bf16[512,128]{1,0:T(8,128)(2,1)} %get-tuple-element.66.refs_15_) | copy-start | bytes 393220
  37.3 8.3 %collective-permute-start = (bf16[512,128]{1,0:T(8,128)(2,1)}, bf16[512,128]{1,0:T(8,128)(2,1)S(1)}, u32[]{:S(2)}, u32[]{:S(2)}) collective-permute-start(bf16[512,128]{1,0:T(8,128)(2,1)} %get-tuple-element.51), channel_id=1, source_target_pairs={{0,15},{1,14},{2,13},{3,12},{4,11},{5,10},{6,9},{7,8},{8,7},{9,6},... | collective-permute-start | bytes 393224 | tf_op jit(solution)/shard_map/ppermute | solution.py:528
  40.3 19.0 %collective-permute-start.1 = (bf16[512,128]{1,0:T(8,128)(2,1)}, bf16[512,128]{1,0:T(8,128)(2,1)S(1)}, u32[]{:S(2)}, u32[]{:S(2)}) collective-permute-start(bf16[512,128]{1,0:T(8,128)(2,1)} %get-tuple-element.52), channel_id=1, source_target_pairs={{0,14},{1,15},{2,12},{3,13},{4,10},{5,11},{6,8},{7,9},{8,6},{9,7},... | collective-permute-start | bytes 393224 | tf_op jit(solution)/shard_map/ppermute | solution.py:528
  41.5 20.3 %collective-permute-start.2 = (bf16[512,128]{1,0:T(8,128)(2,1)}, bf16[512,128]{1,0:T(8,128)(2,1)S(1)}, u32[]{:S(2)}, u32[]{:S(2)}) collective-permute-start(bf16[512,128]{1,0:T(8,128)(2,1)} %get-tuple-element.53), channel_id=1, source_target_pairs={{0,13},{1,12},{2,15},{3,14},{4,9},{5,8},{6,11},{7,10},{8,5},{9,4},... | collective-permute-start | bytes 393224 | tf_op jit(solution)/shard_map/ppermute | solution.py:528
  44.1 25.5 %collective-permute-start.3 = (bf16[512,128]{1,0:T(8,128)(2,1)}, bf16[512,128]{1,0:T(8,128)(2,1)S(1)}, u32[]{:S(2)}, u32[]{:S(2)}) collective-permute-start(bf16[512,128]{1,0:T(8,128)(2,1)} %get-tuple-element.54), channel_id=1, source_target_pairs={{0,12},{1,13},{2,14},{3,15},{4,8},{5,9},{6,10},{7,11},{8,4},{9,5},... | collective-permute-start | bytes 393224 | tf_op jit(solution)/shard_map/ppermute | solution.py:528
  45.6 33.9 %collective-permute-start.4 = (bf16[512,128]{1,0:T(8,128)(2,1)}, bf16[512,128]{1,0:T(8,128)(2,1)S(1)}, u32[]{:S(2)}, u32[]{:S(2)}) collective-permute-start(bf16[512,128]{1,0:T(8,128)(2,1)} %get-tuple-element.55), channel_id=1, source_target_pairs={{0,11},{1,10},{2,9},{3,8},{4,15},{5,14},{6,13},{7,12},{8,3},{9,2},... | collective-permute-start | bytes 393224 | tf_op jit(solution)/shard_map/ppermute | solution.py:528
  59.3 23.0 %collective-permute-start.5 = (bf16[512,128]{1,0:T(8,128)(2,1)}, bf16[512,128]{1,0:T(8,128)(2,1)S(1)}, u32[]{:S(2)}, u32[]{:S(2)}) collective-permute-start(bf16[512,128]{1,0:T(8,128)(2,1)} %get-tuple-element.56), channel_id=1, source_target_pairs={{0,10},{1,11},{2,8},{3,9},{4,14},{5,15},{6,12},{7,13},{8,2},{9,3},... | collective-permute-start | bytes 393224 | tf_op jit(solution)/shard_map/ppermute | solution.py:528
  61.8 23.4 %collective-permute-start.6 = (bf16[512,128]{1,0:T(8,128)(2,1)}, bf16[512,128]{1,0:T(8,128)(2,1)S(1)}, u32[]{:S(2)}, u32[]{:S(2)}) collective-permute-start(bf16[512,128]{1,0:T(8,128)(2,1)} %get-tuple-element.57), channel_id=1, source_target_pairs={{0,9},{1,8},{2,11},{3,10},{4,13},{5,12},{6,15},{7,14},{8,1},{9,0},... | collective-permute-start | bytes 393224 | tf_op jit(solution)/shard_map/ppermute | solution.py:528
  69.6 18.3 %collective-permute-start.7 = (bf16[512,128]{1,0:T(8,128)(2,1)}, bf16[512,128]{1,0:T(8,128)(2,1)S(1)}, u32[]{:S(2)}, u32[]{:S(2)}) collective-permute-start(bf16[512,128]{1,0:T(8,128)(2,1)} %get-tuple-element.58), channel_id=1, source_target_pairs={{0,8},{1,9},{2,10},{3,11},{4,12},{5,13},{6,14},{7,15},{8,0},{9,1},... | collective-permute-start | bytes 393224 | tf_op jit(solution)/shard_map/ppermute | solution.py:528
  79.5 11.3 %collective-permute-start.8 = (bf16[512,128]{1,0:T(8,128)(2,1)}, bf16[512,128]{1,0:T(8,128)(2,1)S(1)}, u32[]{:S(2)}, u32[]{:S(2)}) collective-permute-start(bf16[512,128]{1,0:T(8,128)(2,1)} %get-tuple-element.59), channel_id=1, source_target_pairs={{0,7},{1,6},{2,5},{3,4},{4,3},{5,2},{6,1},{7,0},{8,15},{9,14},{10,... | collective-permute-start | bytes 393224 | tf_op jit(solution)/shard_map/ppermute | solution.py:528
  82.3 11.3 %collective-permute-start.9 = (bf16[512,128]{1,0:T(8,128)(2,1)}, bf16[512,128]{1,0:T(8,128)(2,1)S(1)}, u32[]{:S(2)}, u32[]{:S(2)}) collective-permute-start(bf16[512,128]{1,0:T(8,128)(2,1)} %get-tuple-element.60), channel_id=1, source_target_pairs={{0,6},{1,7},{2,4},{3,5},{4,2},{5,3},{6,0},{7,1},{8,14},{9,15},{10,... | collective-permute-start | bytes 393224 | tf_op jit(solution)/shard_map/ppermute | solution.py:528
  85.2 11.2 %collective-permute-start.10 = (bf16[512,128]{1,0:T(8,128)(2,1)}, bf16[512,128]{1,0:T(8,128)(2,1)S(1)}, u32[]{:S(2)}, u32[]{:S(2)}) collective-permute-start(bf16[512,128]{1,0:T(8,128)(2,1)} %get-tuple-element.61), channel_id=1, source_target_pairs={{0,5},{1,4},{2,7},{3,6},{4,1},{5,0},{6,3},{7,2},{8,13},{9,12},{10,... | collective-permute-start | bytes 393224 | tf_op jit(solution)/shard_map/ppermute | solution.py:528
  88.0 11.2 %collective-permute-start.11 = (bf16[512,128]{1,0:T(8,128)(2,1)}, bf16[512,128]{1,0:T(8,128)(2,1)S(1)}, u32[]{:S(2)}, u32[]{:S(2)}) collective-permute-start(bf16[512,128]{1,0:T(8,128)(2,1)} %get-tuple-element.62), channel_id=1, source_target_pairs={{0,4},{1,5},{2,6},{3,7},{4,0},{5,1},{6,2},{7,3},{8,12},{9,13},{10,... | collective-permute-start | bytes 393224 | tf_op jit(solution)/shard_map/ppermute | solution.py:528
  90.7 8.5 %collective-permute-start.12 = (bf16[512,128]{1,0:T(8,128)(2,1)}, bf16[512,128]{1,0:T(8,128)(2,1)S(1)}, u32[]{:S(2)}, u32[]{:S(2)}) collective-permute-start(bf16[512,128]{1,0:T(8,128)(2,1)} %get-tuple-element.63), channel_id=1, source_target_pairs={{0,3},{1,2},{2,1},{3,0},{4,7},{5,6},{6,5},{7,4},{8,11},{9,10},{10,... | collective-permute-start | bytes 393224 | tf_op jit(solution)/shard_map/ppermute | solution.py:528
  93.5 5.7 %collective-permute-start.13 = (bf16[512,128]{1,0:T(8,128)(2,1)}, bf16[512,128]{1,0:T(8,128)(2,1)S(1)}, u32[]{:S(2)}, u32[]{:S(2)}) collective-permute-start(bf16[512,128]{1,0:T(8,128)(2,1)} %get-tuple-element.64), channel_id=1, source_target_pairs={{0,2},{1,3},{2,0},{3,1},{4,6},{5,7},{6,4},{7,5},{8,10},{9,11},{10,... | collective-permute-start | bytes 393224 | tf_op jit(solution)/shard_map/ppermute | solution.py:528
  94.7 4.4 %collective-permute-start.14 = (bf16[512,128]{1,0:T(8,128)(2,1)}, bf16[512,128]{1,0:T(8,128)(2,1)S(1)}, u32[]{:S(2)}, u32[]{:S(2)}) collective-permute-start(bf16[512,128]{1,0:T(8,128)(2,1)} %get-tuple-element.65), channel_id=1, source_target_pairs={{0,1},{1,0},{2,3},{3,2},{4,5},{5,4},{6,7},{7,6},{8,9},{9,8},{10,11... | collective-permute-start | bytes 393224 | tf_op jit(solution)/shard_map/ppermute | solution.py:528
  96.4 68.0 %collective-permute-start.37 = (bf16[1,4,264,128]{3,2,1,0:T(8,128)(2,1)S(1)}, bf16[1,4,264,128]{3,2,1,0:T(8,128)(2,1)S(1)}, u32[]{:S(2)}, u32[]{:S(2)}) collective-permute-start(bf16[1,4,264,128]{3,2,1,0:T(8,128)(2,1)S(1)} %get-tuple-element.91), channel_id=1, source_target_pairs={{0,2},{1,3},{2,0},{3,1},{4,6},{5,7},{6,4},{7,5},{8,10},{9,11},{10,... | collective-permute-start | bytes 811016 | tf_op jit(solution)/shard_map/ppermute | solution.py:528
  115.7 8.7 %collective-permute-start.15 = (bf16[520,128]{1,0:T(8,128)(2,1)}, bf16[520,128]{1,0:T(8,128)(2,1)S(1)}, u32[]{:S(2)}, u32[]{:S(2)}) collective-permute-start(bf16[520,128]{1,0:T(8,128)(2,1)} %get-tuple-element.67), channel_id=1, source_target_pairs={{0,15},{1,14},{2,13},{3,12},{4,11},{5,10},{6,9},{7,8},{8,7},{9,6},... | collective-permute-start | bytes 399368 | tf_op jit(solution)/shard_map/ppermute | solution.py:528
  119.8 15.6 %collective-permute-start.16 = (bf16[520,128]{1,0:T(8,128)(2,1)}, bf16[520,128]{1,0:T(8,128)(2,1)S(1)}, u32[]{:S(2)}, u32[]{:S(2)}) collective-permute-start(bf16[520,128]{1,0:T(8,128)(2,1)} %get-tuple-element.68), channel_id=1, source_target_pairs={{0,14},{1,15},{2,12},{3,13},{4,10},{5,11},{6,8},{7,9},{8,6},{9,7},... | collective-permute-start | bytes 399368 | tf_op jit(solution)/shard_map/ppermute | solution.py:528
  120.8 16.9 %collective-permute-start.17 = (bf16[520,128]{1,0:T(8,128)(2,1)S(1)}, bf16[520,128]{1,0:T(8,128)(2,1)S(1)}, u32[]{:S(2)}, u32[]{:S(2)}) collective-permute-start(bf16[520,128]{1,0:T(8,128)(2,1)S(1)} %get-tuple-element.69), channel_id=1, source_target_pairs={{0,13},{1,12},{2,15},{3,14},{4,9},{5,8},{6,11},{7,10},{8,5},{9,4},... | collective-permute-start | bytes 399368 | tf_op jit(solution)/shard_map/ppermute | solution.py:528
  122.4 23.5 %collective-permute-start.18 = (bf16[520,128]{1,0:T(8,128)(2,1)S(1)}, bf16[520,128]{1,0:T(8,128)(2,1)S(1)}, u32[]{:S(2)}, u32[]{:S(2)}) collective-permute-start(bf16[520,128]{1,0:T(8,128)(2,1)S(1)} %get-tuple-element.70), channel_id=1, source_target_pairs={{0,12},{1,13},{2,14},{3,15},{4,8},{5,9},{6,10},{7,11},{8,4},{9,5},... | collective-permute-start | bytes 399368 | tf_op jit(solution)/shard_map/ppermute | solution.py:528
  124.3 28.4 %collective-permute-start.19 = (bf16[520,128]{1,0:T(8,128)(2,1)S(1)}, bf16[520,128]{1,0:T(8,128)(2,1)S(1)}, u32[]{:S(2)}, u32[]{:S(2)}) collective-permute-start(bf16[520,128]{1,0:T(8,128)(2,1)S(1)} %get-tuple-element.71), channel_id=1, source_target_pairs={{0,11},{1,10},{2,9},{3,8},{4,15},{5,14},{6,13},{7,12},{8,3},{9,2},... | collective-permute-start | bytes 399368 | tf_op jit(solution)/shard_map/ppermute | solution.py:528
  135.4 24.1 %collective-permute-start.20 = (bf16[520,128]{1,0:T(8,128)(2,1)S(1)}, bf16[520,128]{1,0:T(8,128)(2,1)S(1)}, u32[]{:S(2)}, u32[]{:S(2)}) collective-permute-start(bf16[520,128]{1,0:T(8,128)(2,1)S(1)} %get-tuple-element.72), channel_id=1, source_target_pairs={{0,10},{1,11},{2,8},{3,9},{4,14},{5,15},{6,12},{7,13},{8,2},{9,3},... | collective-permute-start | bytes 399368 | tf_op jit(solution)/shard_map/ppermute | solution.py:528
  137.7 23.9 %collective-permute-start.21 = (bf16[520,128]{1,0:T(8,128)(2,1)S(1)}, bf16[520,128]{1,0:T(8,128)(2,1)S(1)}, u32[]{:S(2)}, u32[]{:S(2)}) collective-permute-start(bf16[520,128]{1,0:T(8,128)(2,1)S(1)} %get-tuple-element.73), channel_id=1, source_target_pairs={{0,9},{1,8},{2,11},{3,10},{4,13},{5,12},{6,15},{7,14},{8,1},{9,0},... | collective-permute-start | bytes 399368 | tf_op jit(solution)/shard_map/ppermute | solution.py:528
  145.9 18.5 %collective-permute-start.22 = (bf16[520,128]{1,0:T(8,128)(2,1)S(1)}, bf16[520,128]{1,0:T(8,128)(2,1)S(1)}, u32[]{:S(2)}, u32[]{:S(2)}) collective-permute-start(bf16[520,128]{1,0:T(8,128)(2,1)S(1)} %get-tuple-element.74), channel_id=1, source_target_pairs={{0,8},{1,9},{2,10},{3,11},{4,12},{5,13},{6,14},{7,15},{8,0},{9,1},... | collective-permute-start | bytes 399368 | tf_op jit(solution)/shard_map/ppermute | solution.py:528
  152.8 14.8 %collective-permute-start.23 = (bf16[520,128]{1,0:T(8,128)(2,1)S(1)}, bf16[520,128]{1,0:T(8,128)(2,1)S(1)}, u32[]{:S(2)}, u32[]{:S(2)}) collective-permute-start(bf16[520,128]{1,0:T(8,128)(2,1)S(1)} %get-tuple-element.75), channel_id=1, source_target_pairs={{0,7},{1,6},{2,5},{3,4},{4,3},{5,2},{6,1},{7,0},{8,15},{9,14},{10,... | collective-permute-start | bytes 399368 | tf_op jit(solution)/shard_map/ppermute | solution.py:528
  159.5 10.9 %collective-permute-start.24 = (bf16[520,128]{1,0:T(8,128)(2,1)S(1)}, bf16[520,128]{1,0:T(8,128)(2,1)S(1)}, u32[]{:S(2)}, u32[]{:S(2)}) collective-permute-start(bf16[520,128]{1,0:T(8,128)(2,1)S(1)} %get-tuple-element.76), channel_id=1, source_target_pairs={{0,6},{1,7},{2,4},{3,5},{4,2},{5,3},{6,0},{7,1},{8,14},{9,15},{10,... | collective-permute-start | bytes 399368 | tf_op jit(solution)/shard_map/ppermute | solution.py:528
  161.5 11.5 %collective-permute-start.25 = (bf16[520,128]{1,0:T(8,128)(2,1)S(1)}, bf16[520,128]{1,0:T(8,128)(2,1)S(1)}, u32[]{:S(2)}, u32[]{:S(2)}) collective-permute-start(bf16[520,128]{1,0:T(8,128)(2,1)S(1)} %get-tuple-element.77), channel_id=1, source_target_pairs={{0,5},{1,4},{2,7},{3,6},{4,1},{5,0},{6,3},{7,2},{8,13},{9,12},{10,... | collective-permute-start | bytes 399368 | tf_op jit(solution)/shard_map/ppermute | solution.py:528
  164.4 11.5 %collective-permute-start.26 = (bf16[520,128]{1,0:T(8,128)(2,1)S(1)}, bf16[520,128]{1,0:T(8,128)(2,1)S(1)}, u32[]{:S(2)}, u32[]{:S(2)}) collective-permute-start(bf16[520,128]{1,0:T(8,128)(2,1)S(1)} %get-tuple-element.78), channel_id=1, source_target_pairs={{0,4},{1,5},{2,6},{3,7},{4,0},{5,1},{6,2},{7,3},{8,12},{9,13},{10,... | collective-permute-start | bytes 399368 | tf_op jit(solution)/shard_map/ppermute | solution.py:528
  164.4 11.5 %collective-permute-start.27 = (bf16[520,128]{1,0:T(8,128)(2,1)S(1)}, bf16[520,128]{1,0:T(8,128)(2,1)S(1)}, u32[]{:S(2)}, u32[]{:S(2)}) collective-permute-start(bf16[520,128]{1,0:T(8,128)(2,1)S(1)} %get-tuple-element.79), channel_id=1, source_target_pairs={{0,3},{1,2},{2,1},{3,0},{4,7},{5,6},{6,5},{7,4},{8,11},{9,10},{10,... | collective-permute-start | bytes 399368 | tf_op jit(solution)/shard_map/ppermute | solution.py:528
  167.5 10.1 %collective-permute-start.28 = (bf16[520,128]{1,0:T(8,128)(2,1)S(1)}, bf16[520,128]{1,0:T(8,128)(2,1)S(1)}, u32[]{:S(2)}, u32[]{:S(2)}) collective-permute-start(bf16[520,128]{1,0:T(8,128)(2,1)S(1)} %get-tuple-element.80), channel_id=1, source_target_pairs={{0,2},{1,3},{2,0},{3,1},{4,6},{5,7},{6,4},{7,5},{8,10},{9,11},{10,... | collective-permute-start | bytes 399368 | tf_op jit(solution)/shard_map/ppermute | solution.py:528
  170.4 7.2 %collective-permute-start.29 = (bf16[520,128]{1,0:T(8,128)(2,1)S(1)}, bf16[520,128]{1,0:T(8,128)(2,1)S(1)}, u32[]{:S(2)}, u32[]{:S(2)}) collective-permute-start(bf16[520,128]{1,0:T(8,128)(2,1)S(1)} %get-tuple-element.81), channel_id=1, source_target_pairs={{0,1},{1,0},{2,3},{3,2},{4,5},{5,4},{6,7},{7,6},{8,9},{9,8},{10,11... | collective-permute-start | bytes 399368 | tf_op jit(solution)/shard_map/ppermute | solution.py:528
  173.0 6.5 %collective-permute-start.38 = (bf16[520,128]{1,0:T(8,128)(2,1)S(1)}, bf16[520,128]{1,0:T(8,128)(2,1)S(1)}, u32[]{:S(2)}, u32[]{:S(2)}) collective-permute-start(bf16[520,128]{1,0:T(8,128)(2,1)S(1)} %get-tuple-element.92), channel_id=1, source_target_pairs={{0,12},{1,13},{2,14},{3,15},{4,8},{5,9},{6,10},{7,11},{8,4},{9,5},... | collective-permute-start | bytes 399368 | tf_op jit(solution)/shard_map/ppermute | solution.py:528
  175.9 10.2 %collective-permute-start.39 = (bf16[520,128]{1,0:T(8,128)(2,1)S(1)}, bf16[520,128]{1,0:T(8,128)(2,1)S(1)}, u32[]{:S(2)}, u32[]{:S(2)}) collective-permute-start(bf16[520,128]{1,0:T(8,128)(2,1)S(1)} %get-tuple-element.93), channel_id=1, source_target_pairs={{0,8},{1,9},{2,10},{3,11},{4,12},{5,13},{6,14},{7,15},{8,0},{9,1},... | collective-permute-start | bytes 399368 | tf_op jit(solution)/shard_map/ppermute | solution.py:528
  175.9 10.2 %collective-permute-start.40 = (bf16[520,128]{1,0:T(8,128)(2,1)S(1)}, bf16[520,128]{1,0:T(8,128)(2,1)S(1)}, u32[]{:S(2)}, u32[]{:S(2)}) collective-permute-start(bf16[520,128]{1,0:T(8,128)(2,1)S(1)} %get-tuple-element.94), channel_id=1, source_target_pairs={{0,4},{1,5},{2,6},{3,7},{4,0},{5,1},{6,2},{7,3},{8,12},{9,13},{10,... | collective-permute-start | bytes 399368 | tf_op jit(solution)/shard_map/ppermute | solution.py:528
where the time goes:
time: 189 us; the launch traced here: 188 us
  starting transfers between devices  91.7 us (49%)
  waiting for transfers between devices  63.7 us (34%)
  Pallas kernels  30 us (16%)
    ppermute x41, starting transfers between devices, shift(): return lax.ppermute(block, 'ctx', [(i, i ^ step) for i in range(devices)])  91.7 us
    ppermute x41, waiting for transfers between devices, shift(): return lax.ppermute(block, 'ctx', [(i, i ^ step) for i in range(devices)])  63.7 us
    pallas_call x1, Pallas kernels, head_shards(): pl.pallas_call(functools.partial(whole_head, devices), in_specs=[SMEM, SM...  16.5 us
    pallas_call x1, Pallas kernels, head_shards(): pl.pallas_call(functools.partial(shared_head, span, planes), in_specs=[SM...  6.09 us
    pallas_call x2, Pallas kernels, pack(): pl.pallas_call(functools.partial(pack_body, start), grid_spec=pltpu.Prefe...  5.35 us
  transfers between devices with their start and end apart: 41, of which 25 were waited for; matrix products, arithmetic and copies ran while one was open for 0% of the time, Pallas kernels for 11%

commit v1 on v0

--- a/solution.py
+++ b/solution.py
@@ -165,7 +165,7 @@
 
 
 LANES = 128
-JOBS = 4
+JOBS = (8, 4, 2, 1)
 SPLITS = 2
 VMEM = pl.BlockSpec(memory_space=pltpu.VMEM)
 SMEM = pl.BlockSpec(memory_space=pltpu.SMEM)
@@ -294,37 +294,42 @@
         results.append((pair, top))
     for index, (_, (score_ref, prob_ref, pair_ref)) in enumerate(zip(jobs, work)):
         pair, top = results[index]
-        raised = jnp.exp2((score_ref[...] - top) * base2)
-        score_ref[...] = raised
-        inverse = 1.0 / jnp.sum(raised, axis=0, keepdims=True)
+        total = jnp.zeros((8, LANES), jnp.float32)
+        for start, size in spans:
+            raised = jnp.exp2((score_ref[start : start + size] - top) * base2)
+            score_ref[start : start + size] = raised
+            total = total + jnp.sum(raised.reshape(size // 8, 8, LANES), axis=0)
+        inverse = 1.0 / jnp.sum(total, axis=0, keepdims=True)
         results[index] = (pair, inverse)
     outs = []
     for index, ((query, grad, listed), (score_ref, prob_ref, pair_ref)) in enumerate(zip(jobs, work)):
         pair, inverse = results[index]
-        weight = score_ref[...] * inverse
-        rounded = weight.astype(jnp.bfloat16)
-        pair_ref[:, LANES:] = rounded
-        score_ref[...] = weight
-        values_t = jnp.concatenate([value_t[tile] for tile in listed], axis=1)
-        out_t = nn(values_t, pair_ref[:fine, LANES:]) + contract(
-            coarse_value, pair_ref[fine:, LANES:], 0, 0
-        )
+        for start, size in spans:
+            weight = score_ref[start : start + size] * inverse
+            pair_ref[start : start + size, LANES:] = weight.astype(jnp.bfloat16)
+            score_ref[start : start + size] = weight
+        out_t = contract(coarse_value, pair_ref[fine:, LANES:], 0, 0)
+        for slot in range(0, SEL, 2):
+            values_t = jnp.concatenate([value_t[tile] for tile in listed[slot : slot + 2]], axis=1)
+            out_t = out_t + nn(values_t, pair_ref[slot * TILE : (slot + 2) * TILE, LANES:])
         out_t = out_t.astype(jnp.bfloat16).astype(jnp.float32)
         dots = jnp.sum(out_t * grad.astype(jnp.float32).T, axis=0, keepdims=True)
         outs.append((out_t, dots))
     for index, ((query, grad, listed), (score_ref, prob_ref, pair_ref)) in enumerate(zip(jobs, work)):
         out_t, dots = outs[index]
-        slope = (score_ref[...] * (prob_ref[...] - dots)).astype(jnp.bfloat16)
-        pair_ref[:, :LANES] = slope
+        for start, size in spans:
+            rows = slice(start, start + size)
+            slope = score_ref[rows] * (prob_ref[rows] - dots)
+            pair_ref[rows, :LANES] = slope.astype(jnp.bfloat16)
         terms = nn(pair_ref[...], results[index][0])
         for tile, (start, size) in zip(listed, spans):
             both_sum[tile] += terms[start : start + size]
         pool_key_sum[...] += terms[fine:, :LANES]
         pool_value_sum[...] += terms[fine:, LANES:]
-        keys_t = jnp.concatenate([key_t[tile] for tile in listed], axis=1)
-        query_t = nn(keys_t, pair_ref[:fine, :LANES]) + contract(
-            coarse_key, pair_ref[fine:, :LANES], 0, 0
-        )
+        query_t = contract(coarse_key, pair_ref[fine:, :LANES], 0, 0)
+        for slot in range(0, SEL, 2):
+            keys_t = jnp.concatenate([key_t[tile] for tile in listed[slot : slot + 2]], axis=1)
+            query_t = query_t + nn(keys_t, pair_ref[slot * TILE : (slot + 2) * TILE, :LANES])
         outs[index] = (
             out_t.T.astype(jnp.bfloat16),
             (query_t.T * scaling).astype(jnp.bfloat16),
@@ -356,7 +361,11 @@
     )
 
 
-def head_scratch(tiles):
+def job_count(queries):
+    return next(count for count in JOBS if queries % count == 0)
+
+
+def head_scratch(tiles, jobs):
     comp = tiles * (TILE // POOL)
     keys = SEL * TILE + comp
     return [
@@ -368,7 +377,7 @@
         pltpu.VMEM((tiles, TILE, 2 * LANES), jnp.float32),
         pltpu.VMEM((comp, LANES), jnp.float32),
         pltpu.VMEM((comp, LANES), jnp.float32),
-    ] + JOBS * [
+    ] + jobs * [
         pltpu.VMEM((keys, LANES), jnp.float32),
         pltpu.VMEM((keys, LANES), jnp.float32),
         pltpu.VMEM((keys, 2 * LANES), jnp.bfloat16),
@@ -377,7 +386,7 @@
 
 def split_scratch(scratch):
     totals, work = scratch[:8], scratch[8:]
-    return totals, [work[3 * job : 3 * job + 3] for job in range(JOBS)]
+    return totals, [work[first : first + 3] for first in range(0, len(work), 3)]
 
 
 def head_cost(queries, keys, moved):
@@ -390,20 +399,21 @@
 
 def every_tile(count, stride, place_ref, sel_ref, query_ref, out_ref, totals, work):
     place = place_ref[0]
+    group = len(work)
 
     def some(first, carry):
         jobs = []
-        for job in range(JOBS):
-            piece = first * JOBS + job
+        for job in range(group):
+            piece = first * group + job
             tile = lax.bitwise_xor(place, piece * stride)
             listed = [lax.bitwise_xor(sel_ref[tile, slot], place) for slot in range(SEL)]
             jobs.append((query_ref[piece, :, :LANES], query_ref[piece, :, LANES:], listed))
         for job, (rows, slopes) in enumerate(some_tiles(jobs, totals, work)):
-            out_ref[first * JOBS + job, :TILE, :] = rows
-            out_ref[first * JOBS + job, TILE : 2 * TILE, :] = slopes
+            out_ref[first * group + job, :TILE, :] = rows
+            out_ref[first * group + job, TILE : 2 * TILE, :] = slopes
         return carry
 
-    lax.fori_loop(0, count // JOBS, some, 0)
+    lax.fori_loop(0, count // group, some, 0)
 
 
 def whole_head(tiles, place_ref, sel_ref, *refs):
@@ -560,7 +570,7 @@
             shape(half, planes, part, LANES),
         ],
         scratch_shapes=[pltpu.VMEM((planes, TILE, 2 * LANES), jnp.bfloat16)]
-        + head_scratch(devices),
+        + head_scratch(devices, job_count(planes)),
         compiler_params=BIG,
         cost_estimate=head_cost(planes * TILE, keys, 16 * devices * TILE * LANES),
         name="shared_head",
@@ -599,7 +609,7 @@
             pltpu.VMEM((devices, TILE, 2 * LANES), jnp.bfloat16),
             pltpu.VMEM((devices, 2 * TILE, LANES), jnp.bfloat16),
         ]
-        + head_scratch(devices),
+        + head_scratch(devices, job_count(devices)),
         compiler_params=BIG,
         cost_estimate=head_cost(devices * TILE, keys, 16 * devices * TILE * LANES),
         name="whole_head",
@@ -621,7 +631,7 @@
     devices = lax.axis_size("ctx")
     planes = HEADS - devices
     tiles_here = query_rows.shape[0] // TILE
-    if planes > 0 and devices % planes == 0 and tiles_here == 1 and planes % JOBS == 0:
+    if planes > 0 and devices % planes == 0 and tiles_here == 1:
         span = devices // planes
         if span & (span - 1) == 0:
             return head_shards(query_rows, key_rows, value_rows, out_grad, selected)

time: 189 us -> 187 us (0.989)
  transfers between devices with their start and end apart: 41 -> 41, of which waited for: 25 -> 25; matrix products, arithmetic and copies ran while one was open for 0% -> 0% of each run, Pallas kernels for 11% -> 10%
where the time goes in v1:
time: 187 us
  starting transfers between devices  91.6 us (49%)
  waiting for transfers between devices  63.7 us (34%)
  Pallas kernels  28.8 us (15%)
    ppermute x41, starting transfers between devices, shift(): return lax.ppermute(block, 'ctx', [(i, i ^ step) for i in range(devices)])  91.6 us
    ppermute x41, waiting for transfers between devices, shift(): return lax.ppermute(block, 'ctx', [(i, i ^ step) for i in range(devices)])  63.7 us
    pallas_call x1, Pallas kernels, head_shards(): pl.pallas_call(functools.partial(whole_head, devices), in_specs=[SMEM, SM...  15.4 us
    pallas_call x1, Pallas kernels, head_shards(): pl.pallas_call(functools.partial(shared_head, span, planes), in_specs=[SM...  5.94 us
    pallas_call x2, Pallas kernels, pack(): pl.pallas_call(functools.partial(pack_body, start), grid_spec=pltpu.Prefe...  5.35 us
  transfers between devices with their start and end apart: 41, of which 25 were waited for; matrix products, arithmetic and copies ran while one was open for 0% of the time, Pallas kernels for 10%

profile of v1, /device:TPU:1, one launch (start us, length us, event | category | flops | bytes accessed | tf_op | source)
XLA Modules:
  0.0 186.7 jit_solution(16635054071072475761)
XLA Ops:
  0.7 2.0 %pack.3 = (bf16[512,128]{1,0:T(8,128)(2,1)}, bf16[512,128]{1,0:T(8,128)(2,1)}, bf16[512,128]{1,0:T(8,128)(2,1)}, bf16[512,128]{1,0:T(8,128)(2,1)}) custom-call(s32[1]{0:T(128)S(6)} %select_n.5.place_ref, bf16[128,2560]{1,0:T(8,128)(2,1)} %q_ref.3, bf16[128,2560]{1,0:T(8,128)(2,1)} %k_ref.3, bf16[128,2560]{1,0:T(8,128)(2,1)} %v_ref.3, bf16[128,2560]{1,0:T(8,128)(2,1)} %g_ref.3), custom_call_target="tpu_custom_call" | custom-call | bytes 1048576 | tf_op jit(solution)/shard_map/pack/pallas_call | solution.py:235
  2.6 2.1 %collective-permute-start.30 = (bf16[512,128]{1,0:T(8,128)(2,1)}, bf16[512,128]{1,0:T(8,128)(2,1)S(1)}, u32[]{:S(2)}, u32[]{:S(2)}) collective-permute-start(bf16[512,128]{1,0:T(8,128)(2,1)} %get-tuple-element.84), channel_id=1, source_target_pairs={{0,4},{1,5},{2,6},{3,7},{4,0},{5,1},{6,2},{7,3},{8,12},{9,13},{10,... | collective-permute-start | bytes 393224 | tf_op jit(solution)/shard_map/ppermute | solution.py:538
  4.8 2.3 %collective-permute-start.31 = (bf16[512,128]{1,0:T(8,128)(2,1)}, bf16[512,128]{1,0:T(8,128)(2,1)S(1)}, u32[]{:S(2)}, u32[]{:S(2)}) collective-permute-start(bf16[512,128]{1,0:T(8,128)(2,1)} %get-tuple-element.85), channel_id=1, source_target_pairs={{0,8},{1,9},{2,10},{3,11},{4,12},{5,13},{6,14},{7,15},{8,0},{9,1},... | collective-permute-start | bytes 393224 | tf_op jit(solution)/shard_map/ppermute | solution.py:538
  8.2 2.2 %collective-permute-done.31.refs_2_ = bf16[512,128]{1,0:T(8,128)(2,1)S(1)} collective-permute-done((bf16[512,128]{1,0:T(8,128)(2,1)}, bf16[512,128]{1,0:T(8,128)(2,1)S(1)}, u32[]{:S(2)}, u32[]{:S(2)}) %collective-permute-start.31) | collective-permute-done | bytes 131104 | tf_op jit(solution)/shard_map/ppermute | solution.py:538
  10.3 5.4 %collective-permute-done.32.refs_3_ = bf16[512,128]{1,0:T(8,128)(2,1)S(1)} collective-permute-done((bf16[512,128]{1,0:T(8,128)(2,1)}, bf16[512,128]{1,0:T(8,128)(2,1)S(1)}, u32[]{:S(2)}, u32[]{:S(2)}) %collective-permute-start.32) | collective-permute-done | bytes 131104 | tf_op jit(solution)/shard_map/ppermute | solution.py:538
  15.8 1.3 collective-permute-start.34
  17.1 3.4 %collective-permute-start.33 = (bf16[4,256,128]{2,1,0:T(8,128)(2,1)S(1)}, bf16[4,256,128]{2,1,0:T(8,128)(2,1)S(1)}, u32[]{:S(2)}, u32[]{:S(2)}) collective-permute-start(bf16[4,256,128]{2,1,0:T(8,128)(2,1)S(1)} %pad_maximum_fusion), channel_id=1, source_target_pairs={{0,1},{1,0},{2,3},{3,2},{4,5},{5,4},{6,7},{7,6},{8,9},{9,8},{10,11... | collective-permute-start | bytes 786440 | tf_op jit(solution)/shard_map/ppermute | solution.py:538
  21.1 4.2 %collective-permute-start.35 = (bf16[4,256,128]{2,1,0:T(8,128)(2,1)S(1)}, bf16[4,256,128]{2,1,0:T(8,128)(2,1)S(1)}, u32[]{:S(2)}, u32[]{:S(2)}) collective-permute-start(bf16[4,256,128]{2,1,0:T(8,128)(2,1)S(1)} %collective-permute-done.34.refs_5_), channel_id=1, source_target_pairs={{0,1},{1,0},{2,3},{3,2},{4,5},{5,4},{6,7},{7,6},{8,9},{9,8},{10,11... | collective-permute-start | bytes 786440 | tf_op jit(solution)/shard_map/ppermute | solution.py:538
  27.4 5.9 %shared_head.1 = (bf16[4,256,128]{2,1,0:T(8,128)(2,1)S(1)}, f32[2,4,264,128]{3,2,1,0:T(8,128)S(1)}, bf16[2,4,264,128]{3,2,1,0:T(8,128)(2,1)S(1)}) custom-call(s32[1]{0:T(128)} %bitcast.place_ref, s32[16,8]{1,0:T(8,128)S(1)} %copy.11.sel_ref, bf16[512,128]{1,0:T(8,128)(2,1)S(1)} %copy-done, bf16[512,128]{1,0:T(8,128)(2,1)S(1)} %collective-permute-done.30.refs_1_, ...), custom_call_target="tpu_custom_call" | custom-call | flops 830472192 | bytes 4194304 | tf_op jit(solution)/shard_map/shared_head/pallas_call | solution.py:563
  33.8 3.4 %pack.2 = (bf16[512,128]{1,0:T(8,128)(2,1)}, bf16[512,128]{1,0:T(8,128)(2,1)}, bf16[512,128]{1,0:T(8,128)(2,1)}, bf16[512,128]{1,0:T(8,128)(2,1)}, bf16[512,128]...) custom-call(s32[1]{0:T(128)} %bitcast.place_ref, ...), custom_call_target="tpu_custom_call" | custom-call | bytes 4194304 | tf_op jit(solution)/shard_map/pack/pallas_call | solution.py:235
  37.1 3.0 %collective-permute-start = (bf16[512,128]{1,0:T(8,128)(2,1)}, bf16[512,128]{1,0:T(8,128)(2,1)S(1)}, u32[]{:S(2)}, u32[]{:S(2)}) collective-permute-start(bf16[512,128]{1,0:T(8,128)(2,1)} %get-tuple-element.51), channel_id=1, source_target_pairs={{0,15},{1,14},{2,13},{3,12},{4,11},{5,10},{6,9},{7,8},{8,7},{9,6},... | collective-permute-start | bytes 393224 | tf_op jit(solution)/shard_map/ppermute | solution.py:538
  40.1 1.3 collective-permute-start.1
  41.4 2.5 %collective-permute-start.2 = (bf16[512,128]{1,0:T(8,128)(2,1)}, bf16[512,128]{1,0:T(8,128)(2,1)S(1)}, u32[]{:S(2)}, u32[]{:S(2)}) collective-permute-start(bf16[512,128]{1,0:T(8,128)(2,1)} %get-tuple-element.53), channel_id=1, source_target_pairs={{0,13},{1,12},{2,15},{3,14},{4,9},{5,8},{6,11},{7,10},{8,5},{9,4},... | collective-permute-start | bytes 393224 | tf_op jit(solution)/shard_map/ppermute | solution.py:538
  43.9 1.3 collective-permute-start.3
  45.5 13.7 %collective-permute-start.4 = (bf16[512,128]{1,0:T(8,128)(2,1)}, bf16[512,128]{1,0:T(8,128)(2,1)S(1)}, u32[]{:S(2)}, u32[]{:S(2)}) collective-permute-start(bf16[512,128]{1,0:T(8,128)(2,1)} %get-tuple-element.55), channel_id=1, source_target_pairs={{0,11},{1,10},{2,9},{3,8},{4,15},{5,14},{6,13},{7,12},{8,3},{9,2},... | collective-permute-start | bytes 393224 | tf_op jit(solution)/shard_map/ppermute | solution.py:538
  59.1 2.5 %collective-permute-start.5 = (bf16[512,128]{1,0:T(8,128)(2,1)}, bf16[512,128]{1,0:T(8,128)(2,1)S(1)}, u32[]{:S(2)}, u32[]{:S(2)}) collective-permute-start(bf16[512,128]{1,0:T(8,128)(2,1)} %get-tuple-element.56), channel_id=1, source_target_pairs={{0,10},{1,11},{2,8},{3,9},{4,14},{5,15},{6,12},{7,13},{8,2},{9,3},... | collective-permute-start | bytes 393224 | tf_op jit(solution)/shard_map/ppermute | solution.py:538
  61.7 7.8 %collective-permute-start.6 = (bf16[512,128]{1,0:T(8,128)(2,1)}, bf16[512,128]{1,0:T(8,128)(2,1)S(1)}, u32[]{:S(2)}, u32[]{:S(2)}) collective-permute-start(bf16[512,128]{1,0:T(8,128)(2,1)} %get-tuple-element.57), channel_id=1, source_target_pairs={{0,9},{1,8},{2,11},{3,10},{4,13},{5,12},{6,15},{7,14},{8,1},{9,0},... | collective-permute-start | bytes 393224 | tf_op jit(solution)/shard_map/ppermute | solution.py:538
  69.5 2.5 %collective-permute-start.7 = (bf16[512,128]{1,0:T(8,128)(2,1)}, bf16[512,128]{1,0:T(8,128)(2,1)S(1)}, u32[]{:S(2)}, u32[]{:S(2)}) collective-permute-start(bf16[512,128]{1,0:T(8,128)(2,1)} %get-tuple-element.58), channel_id=1, source_target_pairs={{0,8},{1,9},{2,10},{3,11},{4,12},{5,13},{6,14},{7,15},{8,0},{9,1},... | collective-permute-start | bytes 393224 | tf_op jit(solution)/shard_map/ppermute | solution.py:538
  72.0 7.3 %collective-permute-done.4.refs_4_ = bf16[512,128]{1,0:T(8,128)(2,1)S(1)} collective-permute-done((bf16[512,128]{1,0:T(8,128)(2,1)}, bf16[512,128]{1,0:T(8,128)(2,1)S(1)}, u32[]{:S(2)}, u32[]{:S(2)}) %collective-permute-start.4) | collective-permute-done | bytes 131104 | tf_op jit(solution)/shard_map/ppermute | solution.py:538
  79.3 2.8 %collective-permute-done.5.refs_5_ = bf16[512,128]{1,0:T(8,128)(2,1)S(1)} collective-permute-done((bf16[512,128]{1,0:T(8,128)(2,1)}, bf16[512,128]{1,0:T(8,128)(2,1)S(1)}, u32[]{:S(2)}, u32[]{:S(2)}) %collective-permute-start.5) | collective-permute-done | bytes 131104 | tf_op jit(solution)/shard_map/ppermute | solution.py:538
  82.1 2.9 %collective-permute-done.6.refs_6_ = bf16[512,128]{1,0:T(8,128)(2,1)S(1)} collective-permute-done((bf16[512,128]{1,0:T(8,128)(2,1)}, bf16[512,128]{1,0:T(8,128)(2,1)S(1)}, u32[]{:S(2)}, u32[]{:S(2)}) %collective-permute-start.6) | collective-permute-done | bytes 131104 | tf_op jit(solution)/shard_map/ppermute | solution.py:538
  85.2 2.6 %collective-permute-done.7.refs_7_ = bf16[512,128]{1,0:T(8,128)(2,1)S(1)} collective-permute-done((bf16[512,128]{1,0:T(8,128)(2,1)}, bf16[512,128]{1,0:T(8,128)(2,1)S(1)}, u32[]{:S(2)}, u32[]{:S(2)}) %collective-permute-start.7) | collective-permute-done | bytes 131104 | tf_op jit(solution)/shard_map/ppermute | solution.py:538
  87.8 2.8 %collective-permute-done.8.refs_8_ = bf16[512,128]{1,0:T(8,128)(2,1)S(1)} collective-permute-done((bf16[512,128]{1,0:T(8,128)(2,1)}, bf16[512,128]{1,0:T(8,128)(2,1)S(1)}, u32[]{:S(2)}, u32[]{:S(2)}) %collective-permute-start.8) | collective-permute-done | bytes 131104 | tf_op jit(solution)/shard_map/ppermute | solution.py:538
  90.6 1.5 collective-permute-start.12
  92.1 1.3 collective-permute-done.9.refs_9_
  93.4 1.2 collective-permute-start.13
  96.5 2.5 %collective-permute-done.11.refs_11_ = bf16[512,128]{1,0:T(8,128)(2,1)S(1)} collective-permute-done((bf16[512,128]{1,0:T(8,128)(2,1)}, bf16[512,128]{1,0:T(8,128)(2,1)S(1)}, u32[]{:S(2)}, u32[]{:S(2)}) %collective-permute-start.11) | collective-permute-done | bytes 131104 | tf_op jit(solution)/shard_map/ppermute | solution.py:538
  99.0 15.4 %whole_head.1 = (bf16[520,128]{1,0:T(8,128)(2,1)S(1)}, bf16[520,128]{1,0:T(8,128)(2,1)S(1)}, bf16[520,128]{1,0:T(8,128)(2,1)S(1)}, bf16[520,128]{1,0:T(8,128)(2,...) custom-call(s32[1]{0:T(128)} %bitcast.place_ref, ...), custom_call_target="tpu_custom_call" | custom-call | flops 3321888768 | bytes 4194304 | tf_op jit(solution)/shard_map/whole_head/pallas_call | solution.py:603
  114.4 4.1 %collective-permute-start.15 = (bf16[520,128]{1,0:T(8,128)(2,1)}, bf16[520,128]{1,0:T(8,128)(2,1)S(1)}, u32[]{:S(2)}, u32[]{:S(2)}) collective-permute-start(bf16[520,128]{1,0:T(8,128)(2,1)} %get-tuple-element.67), channel_id=1, source_target_pairs={{0,15},{1,14},{2,13},{3,12},{4,11},{5,10},{6,9},{7,8},{8,7},{9,6},... | collective-permute-start | bytes 399368 | tf_op jit(solution)/shard_map/ppermute | solution.py:538
  119.6 1.5 collective-permute-start.17
  121.1 1.3 collective-permute-start.18
  123.1 11.0 %collective-permute-start.19 = (bf16[520,128]{1,0:T(8,128)(2,1)S(1)}, bf16[520,128]{1,0:T(8,128)(2,1)S(1)}, u32[]{:S(2)}, u32[]{:S(2)}) collective-permute-start(bf16[520,128]{1,0:T(8,128)(2,1)S(1)} %get-tuple-element.71), channel_id=1, source_target_pairs={{0,11},{1,10},{2,9},{3,8},{4,15},{5,14},{6,13},{7,12},{8,3},{9,2},... | collective-permute-start | bytes 399368 | tf_op jit(solution)/shard_map/ppermute | solution.py:538
  134.1 2.3 %collective-permute-start.20 = (bf16[520,128]{1,0:T(8,128)(2,1)S(1)}, bf16[520,128]{1,0:T(8,128)(2,1)S(1)}, u32[]{:S(2)}, u32[]{:S(2)}) collective-permute-start(bf16[520,128]{1,0:T(8,128)(2,1)S(1)} %get-tuple-element.72), channel_id=1, source_target_pairs={{0,10},{1,11},{2,8},{3,9},{4,14},{5,15},{6,12},{7,13},{8,2},{9,3},... | collective-permute-start | bytes 399368 | tf_op jit(solution)/shard_map/ppermute | solution.py:538
  136.4 8.2 %collective-permute-start.21 = (bf16[520,128]{1,0:T(8,128)(2,1)S(1)}, bf16[520,128]{1,0:T(8,128)(2,1)S(1)}, u32[]{:S(2)}, u32[]{:S(2)}) collective-permute-start(bf16[520,128]{1,0:T(8,128)(2,1)S(1)} %get-tuple-element.73), channel_id=1, source_target_pairs={{0,9},{1,8},{2,11},{3,10},{4,13},{5,12},{6,15},{7,14},{8,1},{9,0},... | collective-permute-start | bytes 399368 | tf_op jit(solution)/shard_map/ppermute | solution.py:538
  144.6 5.1 %collective-permute-start.22 = (bf16[520,128]{1,0:T(8,128)(2,1)S(1)}, bf16[520,128]{1,0:T(8,128)(2,1)S(1)}, u32[]{:S(2)}, u32[]{:S(2)}) collective-permute-start(bf16[520,128]{1,0:T(8,128)(2,1)S(1)} %get-tuple-element.74), channel_id=1, source_target_pairs={{0,8},{1,9},{2,10},{3,11},{4,12},{5,13},{6,14},{7,15},{8,0},{9,1},... | collective-permute-start | bytes 399368 | tf_op jit(solution)/shard_map/ppermute | solution.py:538
  149.8 1.7 collective-permute-done.19.refs_4_
  151.5 6.8 %collective-permute-done.20.refs_5_ = bf16[520,128]{1,0:T(8,128)(2,1)S(1)} collective-permute-done((bf16[520,128]{1,0:T(8,128)(2,1)S(1)}, bf16[520,128]{1,0:T(8,128)(2,1)S(1)}, u32[]{:S(2)}, u32[]{:S(2)}) %collective-permute-start.20) | collective-permute-done | bytes 133152 | tf_op jit(solution)/shard_map/ppermute | solution.py:538
  158.3 2.0 %collective-permute-done.21.refs_6_ = bf16[520,128]{1,0:T(8,128)(2,1)S(1)} collective-permute-done((bf16[520,128]{1,0:T(8,128)(2,1)S(1)}, bf16[520,128]{1,0:T(8,128)(2,1)S(1)}, u32[]{:S(2)}, u32[]{:S(2)}) %collective-permute-start.21) | collective-permute-done | bytes 133152 | tf_op jit(solution)/shard_map/ppermute | solution.py:538
  160.3 2.8 %collective-permute-done.22.refs_7_ = bf16[520,128]{1,0:T(8,128)(2,1)S(1)} collective-permute-done((bf16[520,128]{1,0:T(8,128)(2,1)S(1)}, bf16[520,128]{1,0:T(8,128)(2,1)S(1)}, u32[]{:S(2)}, u32[]{:S(2)}) %collective-permute-start.22) | collective-permute-done | bytes 133152 | tf_op jit(solution)/shard_map/ppermute | solution.py:538
  163.6 2.6 %collective-permute-done.23.refs_8_ = bf16[520,128]{1,0:T(8,128)(2,1)S(1)} collective-permute-done((bf16[520,128]{1,0:T(8,128)(2,1)S(1)}, bf16[520,128]{1,0:T(8,128)(2,1)S(1)}, u32[]{:S(2)}, u32[]{:S(2)}) %collective-permute-start.23) | collective-permute-done | bytes 133152 | tf_op jit(solution)/shard_map/ppermute | solution.py:538
  167.2 2.0 %collective-permute-done.24.refs_9_ = bf16[520,128]{1,0:T(8,128)(2,1)S(1)} collective-permute-done((bf16[520,128]{1,0:T(8,128)(2,1)S(1)}, bf16[520,128]{1,0:T(8,128)(2,1)S(1)}, u32[]{:S(2)}, u32[]{:S(2)}) %collective-permute-start.24) | collective-permute-done | bytes 133152 | tf_op jit(solution)/shard_map/ppermute | solution.py:538
  169.6 2.2 %collective-permute-done.25.refs_10_ = bf16[520,128]{1,0:T(8,128)(2,1)S(1)} collective-permute-done((bf16[520,128]{1,0:T(8,128)(2,1)S(1)}, bf16[520,128]{1,0:T(8,128)(2,1)S(1)}, u32[]{:S(2)}, u32[]{:S(2)}) %collective-permute-start.25) | collective-permute-done | bytes 133152 | tf_op jit(solution)/shard_map/ppermute | solution.py:538
  171.8 1.3 collective-permute-start.38
  173.1 1.5 collective-permute-done.26.refs_11_
  174.6 1.7 collective-permute-start.40
  176.3 2.0 %collective-permute-done.38.refs_16_ = bf16[520,128]{1,0:T(8,128)(2,1)S(1)} collective-permute-done((bf16[520,128]{1,0:T(8,128)(2,1)S(1)}, bf16[520,128]{1,0:T(8,128)(2,1)S(1)}, u32[]{:S(2)}, u32[]{:S(2)}) %collective-permute-start.38) | collective-permute-done | bytes 133152 | tf_op jit(solution)/shard_map/ppermute | solution.py:538
  178.3 6.5 %collective-permute-done.39.refs_17_ = bf16[520,128]{1,0:T(8,128)(2,1)S(1)} collective-permute-done((bf16[520,128]{1,0:T(8,128)(2,1)S(1)}, bf16[520,128]{1,0:T(8,128)(2,1)S(1)}, u32[]{:S(2)}, u32[]{:S(2)}) %collective-permute-start.39) | collective-permute-done | bytes 133152 | tf_op jit(solution)/shard_map/ppermute | solution.py:538
  184.8 2.0 %unpack.1 = (bf16[128,2560]{1,0:T(8,128)(2,1)}, bf16[128,2560]{1,0:T(8,128)(2,1)}, bf16[128,2560]{1,0:T(8,128)(2,1)}, bf16[128,2560]{1,0:T(8,128)(2,1)}, f32[2,2560]{1,0:T(2,128)}, /*index=5*/f32[2,2560]{1,0:T(2,128)}) custom-call(s32[1]{0:T(128)} %bitcast.place_ref, bf16[520,128]{1,0:T(8,128)(2,1)S(1)} %collective-permute-done.15.refs_0_, ...), custom_call_target="tpu_custom_call" | custom-call | tf_op jit(solution)/shard_map/unpack/pallas_call | solution.py:620
  (53 shorter events, 10.3 us)
Async XLA Ops:
  0.6 24.7 %copy-start.2 = (s32[16,8]{0,1:T(8,128)S(1)}, s32[16,8]{0,1:T(8,128)}, u32[]{:S(2)}) copy-start(s32[16,8]{0,1:T(8,128)} %param.9) | copy-start | bytes 1540
  2.6 5.5 %collective-permute-start.30 = (bf16[512,128]{1,0:T(8,128)(2,1)}, bf16[512,128]{1,0:T(8,128)(2,1)S(1)}, u32[]{:S(2)}, u32[]{:S(2)}) collective-permute-start(bf16[512,128]{1,0:T(8,128)(2,1)} %get-tuple-element.84), channel_id=1, source_target_pairs={{0,4},{1,5},{2,6},{3,7},{4,0},{5,1},{6,2},{7,3},{8,12},{9,13},{10,... | collective-permute-start | bytes 393224 | tf_op jit(solution)/shard_map/ppermute | solution.py:538
  4.8 5.6 %collective-permute-start.31 = (bf16[512,128]{1,0:T(8,128)(2,1)}, bf16[512,128]{1,0:T(8,128)(2,1)S(1)}, u32[]{:S(2)}, u32[]{:S(2)}) collective-permute-start(bf16[512,128]{1,0:T(8,128)(2,1)} %get-tuple-element.85), channel_id=1, source_target_pairs={{0,8},{1,9},{2,10},{3,11},{4,12},{5,13},{6,14},{7,15},{8,0},{9,1},... | collective-permute-start | bytes 393224 | tf_op jit(solution)/shard_map/ppermute | solution.py:538
  7.1 8.7 %collective-permute-start.32 = (bf16[512,128]{1,0:T(8,128)(2,1)}, bf16[512,128]{1,0:T(8,128)(2,1)S(1)}, u32[]{:S(2)}, u32[]{:S(2)}) collective-permute-start(bf16[512,128]{1,0:T(8,128)(2,1)} %get-tuple-element.86), channel_id=1, source_target_pairs={{0,12},{1,13},{2,14},{3,15},{4,8},{5,9},{6,10},{7,11},{8,4},{9,5},... | collective-permute-start | bytes 393224 | tf_op jit(solution)/shard_map/ppermute | solution.py:538
  15.8 5.3 %collective-permute-start.34 = (bf16[4,256,128]{2,1,0:T(8,128)(2,1)S(1)}, bf16[4,256,128]{2,1,0:T(8,128)(2,1)S(1)}, u32[]{:S(2)}, u32[]{:S(2)}) collective-permute-start(bf16[4,256,128]{2,1,0:T(8,128)(2,1)S(1)} %pad_maximum_fusion), channel_id=1, source_target_pairs={{0,2},{1,3},{2,0},{3,1},{4,6},{5,7},{6,4},{7,5},{8,10},{9,11},{10,... | collective-permute-start | bytes 786440 | tf_op jit(solution)/shard_map/ppermute | solution.py:538
  17.1 8.3 %collective-permute-start.33 = (bf16[4,256,128]{2,1,0:T(8,128)(2,1)S(1)}, bf16[4,256,128]{2,1,0:T(8,128)(2,1)S(1)}, u32[]{:S(2)}, u32[]{:S(2)}) collective-permute-start(bf16[4,256,128]{2,1,0:T(8,128)(2,1)S(1)} %pad_maximum_fusion), channel_id=1, source_target_pairs={{0,1},{1,0},{2,3},{3,2},{4,5},{5,4},{6,7},{7,6},{8,9},{9,8},{10,11... | collective-permute-start | bytes 786440 | tf_op jit(solution)/shard_map/ppermute | solution.py:538
  21.1 5.4 %collective-permute-start.35 = (bf16[4,256,128]{2,1,0:T(8,128)(2,1)S(1)}, bf16[4,256,128]{2,1,0:T(8,128)(2,1)S(1)}, u32[]{:S(2)}, u32[]{:S(2)}) collective-permute-start(bf16[4,256,128]{2,1,0:T(8,128)(2,1)S(1)} %collective-permute-done.34.refs_5_), channel_id=1, source_target_pairs={{0,1},{1,0},{2,3},{3,2},{4,5},{5,4},{6,7},{7,6},{8,9},{9,8},{10,11... | collective-permute-start | bytes 786440 | tf_op jit(solution)/shard_map/ppermute | solution.py:538
  26.5 0.9 copy-start
  33.3 61.3 %collective-permute-start.36 = (bf16[2,4,264,128]{3,2,1,0:T(8,128)(2,1)S(1)}, bf16[2,4,264,128]{3,2,1,0:T(8,128)(2,1)S(1)}, u32[]{:S(2)}, u32[]{:S(2)}) collective-permute-start(bf16[2,4,264,128]{3,2,1,0:T(8,128)(2,1)S(1)} %get-tuple-element.89), channel_id=1, source_target_pairs={{0,1},{1,0},{2,3},{3,2},{4,5},{5,4},{6,7},{7,6},{8,9},{9,8},{10,11... | collective-permute-start | bytes 1622024 | tf_op jit(solution)/shard_map/ppermute | solution.py:538
  37.1 61.9 %copy-start.1 = (bf16[512,128]{1,0:T(8,128)(2,1)S(1)}, bf16[512,128]{1,0:T(8,128)(2,1)}, u32[]{:S(2)}) copy-start(bf16[512,128]{1,0:T(8,128)(2,1)} %get-tuple-element.66.refs_15_) | copy-start | bytes 393220
  37.1 8.3 %collective-permute-start = (bf16[512,128]{1,0:T(8,128)(2,1)}, bf16[512,128]{1,0:T(8,128)(2,1)S(1)}, u32[]{:S(2)}, u32[]{:S(2)}) collective-permute-start(bf16[512,128]{1,0:T(8,128)(2,1)} %get-tuple-element.51), channel_id=1, source_target_pairs={{0,15},{1,14},{2,13},{3,12},{4,11},{5,10},{6,9},{7,8},{8,7},{9,6},... | collective-permute-start | bytes 393224 | tf_op jit(solution)/shard_map/ppermute | solution.py:538
  40.1 19.0 %collective-permute-start.1 = (bf16[512,128]{1,0:T(8,128)(2,1)}, bf16[512,128]{1,0:T(8,128)(2,1)S(1)}, u32[]{:S(2)}, u32[]{:S(2)}) collective-permute-start(bf16[512,128]{1,0:T(8,128)(2,1)} %get-tuple-element.52), channel_id=1, source_target_pairs={{0,14},{1,15},{2,12},{3,13},{4,10},{5,11},{6,8},{7,9},{8,6},{9,7},... | collective-permute-start | bytes 393224 | tf_op jit(solution)/shard_map/ppermute | solution.py:538
  41.4 20.3 %collective-permute-start.2 = (bf16[512,128]{1,0:T(8,128)(2,1)}, bf16[512,128]{1,0:T(8,128)(2,1)S(1)}, u32[]{:S(2)}, u32[]{:S(2)}) collective-permute-start(bf16[512,128]{1,0:T(8,128)(2,1)} %get-tuple-element.53), channel_id=1, source_target_pairs={{0,13},{1,12},{2,15},{3,14},{4,9},{5,8},{6,11},{7,10},{8,5},{9,4},... | collective-permute-start | bytes 393224 | tf_op jit(solution)/shard_map/ppermute | solution.py:538
  43.9 25.5 %collective-permute-start.3 = (bf16[512,128]{1,0:T(8,128)(2,1)}, bf16[512,128]{1,0:T(8,128)(2,1)S(1)}, u32[]{:S(2)}, u32[]{:S(2)}) collective-permute-start(bf16[512,128]{1,0:T(8,128)(2,1)} %get-tuple-element.54), channel_id=1, source_target_pairs={{0,12},{1,13},{2,14},{3,15},{4,8},{5,9},{6,10},{7,11},{8,4},{9,5},... | collective-permute-start | bytes 393224 | tf_op jit(solution)/shard_map/ppermute | solution.py:538
  45.5 33.9 %collective-permute-start.4 = (bf16[512,128]{1,0:T(8,128)(2,1)}, bf16[512,128]{1,0:T(8,128)(2,1)S(1)}, u32[]{:S(2)}, u32[]{:S(2)}) collective-permute-start(bf16[512,128]{1,0:T(8,128)(2,1)} %get-tuple-element.55), channel_id=1, source_target_pairs={{0,11},{1,10},{2,9},{3,8},{4,15},{5,14},{6,13},{7,12},{8,3},{9,2},... | collective-permute-start | bytes 393224 | tf_op jit(solution)/shard_map/ppermute | solution.py:538
  59.1 23.0 %collective-permute-start.5 = (bf16[512,128]{1,0:T(8,128)(2,1)}, bf16[512,128]{1,0:T(8,128)(2,1)S(1)}, u32[]{:S(2)}, u32[]{:S(2)}) collective-permute-start(bf16[512,128]{1,0:T(8,128)(2,1)} %get-tuple-element.56), channel_id=1, source_target_pairs={{0,10},{1,11},{2,8},{3,9},{4,14},{5,15},{6,12},{7,13},{8,2},{9,3},... | collective-permute-start | bytes 393224 | tf_op jit(solution)/shard_map/ppermute | solution.py:538
  61.7 23.4 %collective-permute-start.6 = (bf16[512,128]{1,0:T(8,128)(2,1)}, bf16[512,128]{1,0:T(8,128)(2,1)S(1)}, u32[]{:S(2)}, u32[]{:S(2)}) collective-permute-start(bf16[512,128]{1,0:T(8,128)(2,1)} %get-tuple-element.57), channel_id=1, source_target_pairs={{0,9},{1,8},{2,11},{3,10},{4,13},{5,12},{6,15},{7,14},{8,1},{9,0},... | collective-permute-start | bytes 393224 | tf_op jit(solution)/shard_map/ppermute | solution.py:538
  69.5 18.3 %collective-permute-start.7 = (bf16[512,128]{1,0:T(8,128)(2,1)}, bf16[512,128]{1,0:T(8,128)(2,1)S(1)}, u32[]{:S(2)}, u32[]{:S(2)}) collective-permute-start(bf16[512,128]{1,0:T(8,128)(2,1)} %get-tuple-element.58), channel_id=1, source_target_pairs={{0,8},{1,9},{2,10},{3,11},{4,12},{5,13},{6,14},{7,15},{8,0},{9,1},... | collective-permute-start | bytes 393224 | tf_op jit(solution)/shard_map/ppermute | solution.py:538
  79.3 11.3 %collective-permute-start.8 = (bf16[512,128]{1,0:T(8,128)(2,1)}, bf16[512,128]{1,0:T(8,128)(2,1)S(1)}, u32[]{:S(2)}, u32[]{:S(2)}) collective-permute-start(bf16[512,128]{1,0:T(8,128)(2,1)} %get-tuple-element.59), channel_id=1, source_target_pairs={{0,7},{1,6},{2,5},{3,4},{4,3},{5,2},{6,1},{7,0},{8,15},{9,14},{10,... | collective-permute-start | bytes 393224 | tf_op jit(solution)/shard_map/ppermute | solution.py:538
  82.1 11.3 %collective-permute-start.9 = (bf16[512,128]{1,0:T(8,128)(2,1)}, bf16[512,128]{1,0:T(8,128)(2,1)S(1)}, u32[]{:S(2)}, u32[]{:S(2)}) collective-permute-start(bf16[512,128]{1,0:T(8,128)(2,1)} %get-tuple-element.60), channel_id=1, source_target_pairs={{0,6},{1,7},{2,4},{3,5},{4,2},{5,3},{6,0},{7,1},{8,14},{9,15},{10,... | collective-permute-start | bytes 393224 | tf_op jit(solution)/shard_map/ppermute | solution.py:538
  85.1 11.2 %collective-permute-start.10 = (bf16[512,128]{1,0:T(8,128)(2,1)}, bf16[512,128]{1,0:T(8,128)(2,1)S(1)}, u32[]{:S(2)}, u32[]{:S(2)}) collective-permute-start(bf16[512,128]{1,0:T(8,128)(2,1)} %get-tuple-element.61), channel_id=1, source_target_pairs={{0,5},{1,4},{2,7},{3,6},{4,1},{5,0},{6,3},{7,2},{8,13},{9,12},{10,... | collective-permute-start | bytes 393224 | tf_op jit(solution)/shard_map/ppermute | solution.py:538
  87.8 11.2 %collective-permute-start.11 = (bf16[512,128]{1,0:T(8,128)(2,1)}, bf16[512,128]{1,0:T(8,128)(2,1)S(1)}, u32[]{:S(2)}, u32[]{:S(2)}) collective-permute-start(bf16[512,128]{1,0:T(8,128)(2,1)} %get-tuple-element.62), channel_id=1, source_target_pairs={{0,4},{1,5},{2,6},{3,7},{4,0},{5,1},{6,2},{7,3},{8,12},{9,13},{10,... | collective-permute-start | bytes 393224 | tf_op jit(solution)/shard_map/ppermute | solution.py:538
  90.6 8.5 %collective-permute-start.12 = (bf16[512,128]{1,0:T(8,128)(2,1)}, bf16[512,128]{1,0:T(8,128)(2,1)S(1)}, u32[]{:S(2)}, u32[]{:S(2)}) collective-permute-start(bf16[512,128]{1,0:T(8,128)(2,1)} %get-tuple-element.63), channel_id=1, source_target_pairs={{0,3},{1,2},{2,1},{3,0},{4,7},{5,6},{6,5},{7,4},{8,11},{9,10},{10,... | collective-permute-start | bytes 393224 | tf_op jit(solution)/shard_map/ppermute | solution.py:538
  93.4 5.6 %collective-permute-start.13 = (bf16[512,128]{1,0:T(8,128)(2,1)}, bf16[512,128]{1,0:T(8,128)(2,1)S(1)}, u32[]{:S(2)}, u32[]{:S(2)}) collective-permute-start(bf16[512,128]{1,0:T(8,128)(2,1)} %get-tuple-element.64), channel_id=1, source_target_pairs={{0,2},{1,3},{2,0},{3,1},{4,6},{5,7},{6,4},{7,5},{8,10},{9,11},{10,... | collective-permute-start | bytes 393224 | tf_op jit(solution)/shard_map/ppermute | solution.py:538
  94.6 4.4 %collective-permute-start.14 = (bf16[512,128]{1,0:T(8,128)(2,1)}, bf16[512,128]{1,0:T(8,128)(2,1)S(1)}, u32[]{:S(2)}, u32[]{:S(2)}) collective-permute-start(bf16[512,128]{1,0:T(8,128)(2,1)} %get-tuple-element.65), channel_id=1, source_target_pairs={{0,1},{1,0},{2,3},{3,2},{4,5},{5,4},{6,7},{7,6},{8,9},{9,8},{10,11... | collective-permute-start | bytes 393224 | tf_op jit(solution)/shard_map/ppermute | solution.py:538
  96.3 66.9 %collective-permute-start.37 = (bf16[1,4,264,128]{3,2,1,0:T(8,128)(2,1)S(1)}, bf16[1,4,264,128]{3,2,1,0:T(8,128)(2,1)S(1)}, u32[]{:S(2)}, u32[]{:S(2)}) collective-permute-start(bf16[1,4,264,128]{3,2,1,0:T(8,128)(2,1)S(1)} %get-tuple-element.91), channel_id=1, source_target_pairs={{0,2},{1,3},{2,0},{3,1},{4,6},{5,7},{6,4},{7,5},{8,10},{9,11},{10,... | collective-permute-start | bytes 811016 | tf_op jit(solution)/shard_map/ppermute | solution.py:538
  114.4 8.7 %collective-permute-start.15 = (bf16[520,128]{1,0:T(8,128)(2,1)}, bf16[520,128]{1,0:T(8,128)(2,1)S(1)}, u32[]{:S(2)}, u32[]{:S(2)}) collective-permute-start(bf16[520,128]{1,0:T(8,128)(2,1)} %get-tuple-element.67), channel_id=1, source_target_pairs={{0,15},{1,14},{2,13},{3,12},{4,11},{5,10},{6,9},{7,8},{8,7},{9,6},... | collective-permute-start | bytes 399368 | tf_op jit(solution)/shard_map/ppermute | solution.py:538
  118.5 15.6 %collective-permute-start.16 = (bf16[520,128]{1,0:T(8,128)(2,1)}, bf16[520,128]{1,0:T(8,128)(2,1)S(1)}, u32[]{:S(2)}, u32[]{:S(2)}) collective-permute-start(bf16[520,128]{1,0:T(8,128)(2,1)} %get-tuple-element.68), channel_id=1, source_target_pairs={{0,14},{1,15},{2,12},{3,13},{4,10},{5,11},{6,8},{7,9},{8,6},{9,7},... | collective-permute-start | bytes 399368 | tf_op jit(solution)/shard_map/ppermute | solution.py:538
  119.6 16.8 %collective-permute-start.17 = (bf16[520,128]{1,0:T(8,128)(2,1)S(1)}, bf16[520,128]{1,0:T(8,128)(2,1)S(1)}, u32[]{:S(2)}, u32[]{:S(2)}) collective-permute-start(bf16[520,128]{1,0:T(8,128)(2,1)S(1)} %get-tuple-element.69), channel_id=1, source_target_pairs={{0,13},{1,12},{2,15},{3,14},{4,9},{5,8},{6,11},{7,10},{8,5},{9,4},... | collective-permute-start | bytes 399368 | tf_op jit(solution)/shard_map/ppermute | solution.py:538
  121.1 23.5 %collective-permute-start.18 = (bf16[520,128]{1,0:T(8,128)(2,1)S(1)}, bf16[520,128]{1,0:T(8,128)(2,1)S(1)}, u32[]{:S(2)}, u32[]{:S(2)}) collective-permute-start(bf16[520,128]{1,0:T(8,128)(2,1)S(1)} %get-tuple-element.70), channel_id=1, source_target_pairs={{0,12},{1,13},{2,14},{3,15},{4,8},{5,9},{6,10},{7,11},{8,4},{9,5},... | collective-permute-start | bytes 399368 | tf_op jit(solution)/shard_map/ppermute | solution.py:538
  123.1 28.4 %collective-permute-start.19 = (bf16[520,128]{1,0:T(8,128)(2,1)S(1)}, bf16[520,128]{1,0:T(8,128)(2,1)S(1)}, u32[]{:S(2)}, u32[]{:S(2)}) collective-permute-start(bf16[520,128]{1,0:T(8,128)(2,1)S(1)} %get-tuple-element.71), channel_id=1, source_target_pairs={{0,11},{1,10},{2,9},{3,8},{4,15},{5,14},{6,13},{7,12},{8,3},{9,2},... | collective-permute-start | bytes 399368 | tf_op jit(solution)/shard_map/ppermute | solution.py:538
  134.1 24.1 %collective-permute-start.20 = (bf16[520,128]{1,0:T(8,128)(2,1)S(1)}, bf16[520,128]{1,0:T(8,128)(2,1)S(1)}, u32[]{:S(2)}, u32[]{:S(2)}) collective-permute-start(bf16[520,128]{1,0:T(8,128)(2,1)S(1)} %get-tuple-element.72), channel_id=1, source_target_pairs={{0,10},{1,11},{2,8},{3,9},{4,14},{5,15},{6,12},{7,13},{8,2},{9,3},... | collective-permute-start | bytes 399368 | tf_op jit(solution)/shard_map/ppermute | solution.py:538
  136.4 23.9 %collective-permute-start.21 = (bf16[520,128]{1,0:T(8,128)(2,1)S(1)}, bf16[520,128]{1,0:T(8,128)(2,1)S(1)}, u32[]{:S(2)}, u32[]{:S(2)}) collective-permute-start(bf16[520,128]{1,0:T(8,128)(2,1)S(1)} %get-tuple-element.73), channel_id=1, source_target_pairs={{0,9},{1,8},{2,11},{3,10},{4,13},{5,12},{6,15},{7,14},{8,1},{9,0},... | collective-permute-start | bytes 399368 | tf_op jit(solution)/shard_map/ppermute | solution.py:538
  144.6 18.5 %collective-permute-start.22 = (bf16[520,128]{1,0:T(8,128)(2,1)S(1)}, bf16[520,128]{1,0:T(8,128)(2,1)S(1)}, u32[]{:S(2)}, u32[]{:S(2)}) collective-permute-start(bf16[520,128]{1,0:T(8,128)(2,1)S(1)} %get-tuple-element.74), channel_id=1, source_target_pairs={{0,8},{1,9},{2,10},{3,11},{4,12},{5,13},{6,14},{7,15},{8,0},{9,1},... | collective-permute-start | bytes 399368 | tf_op jit(solution)/shard_map/ppermute | solution.py:538
  151.5 14.8 %collective-permute-start.23 = (bf16[520,128]{1,0:T(8,128)(2,1)S(1)}, bf16[520,128]{1,0:T(8,128)(2,1)S(1)}, u32[]{:S(2)}, u32[]{:S(2)}) collective-permute-start(bf16[520,128]{1,0:T(8,128)(2,1)S(1)} %get-tuple-element.75), channel_id=1, source_target_pairs={{0,7},{1,6},{2,5},{3,4},{4,3},{5,2},{6,1},{7,0},{8,15},{9,14},{10,... | collective-permute-start | bytes 399368 | tf_op jit(solution)/shard_map/ppermute | solution.py:538
  158.2 10.9 %collective-permute-start.24 = (bf16[520,128]{1,0:T(8,128)(2,1)S(1)}, bf16[520,128]{1,0:T(8,128)(2,1)S(1)}, u32[]{:S(2)}, u32[]{:S(2)}) collective-permute-start(bf16[520,128]{1,0:T(8,128)(2,1)S(1)} %get-tuple-element.76), channel_id=1, source_target_pairs={{0,6},{1,7},{2,4},{3,5},{4,2},{5,3},{6,0},{7,1},{8,14},{9,15},{10,... | collective-permute-start | bytes 399368 | tf_op jit(solution)/shard_map/ppermute | solution.py:538
  160.3 11.5 %collective-permute-start.25 = (bf16[520,128]{1,0:T(8,128)(2,1)S(1)}, bf16[520,128]{1,0:T(8,128)(2,1)S(1)}, u32[]{:S(2)}, u32[]{:S(2)}) collective-permute-start(bf16[520,128]{1,0:T(8,128)(2,1)S(1)} %get-tuple-element.77), channel_id=1, source_target_pairs={{0,5},{1,4},{2,7},{3,6},{4,1},{5,0},{6,3},{7,2},{8,13},{9,12},{10,... | collective-permute-start | bytes 399368 | tf_op jit(solution)/shard_map/ppermute | solution.py:538
  163.2 11.5 %collective-permute-start.26 = (bf16[520,128]{1,0:T(8,128)(2,1)S(1)}, bf16[520,128]{1,0:T(8,128)(2,1)S(1)}, u32[]{:S(2)}, u32[]{:S(2)}) collective-permute-start(bf16[520,128]{1,0:T(8,128)(2,1)S(1)} %get-tuple-element.78), channel_id=1, source_target_pairs={{0,4},{1,5},{2,6},{3,7},{4,0},{5,1},{6,2},{7,3},{8,12},{9,13},{10,... | collective-permute-start | bytes 399368 | tf_op jit(solution)/shard_map/ppermute | solution.py:538
  163.2 11.5 %collective-permute-start.27 = (bf16[520,128]{1,0:T(8,128)(2,1)S(1)}, bf16[520,128]{1,0:T(8,128)(2,1)S(1)}, u32[]{:S(2)}, u32[]{:S(2)}) collective-permute-start(bf16[520,128]{1,0:T(8,128)(2,1)S(1)} %get-tuple-element.79), channel_id=1, source_target_pairs={{0,3},{1,2},{2,1},{3,0},{4,7},{5,6},{6,5},{7,4},{8,11},{9,10},{10,... | collective-permute-start | bytes 399368 | tf_op jit(solution)/shard_map/ppermute | solution.py:538
  166.3 10.1 %collective-permute-start.28 = (bf16[520,128]{1,0:T(8,128)(2,1)S(1)}, bf16[520,128]{1,0:T(8,128)(2,1)S(1)}, u32[]{:S(2)}, u32[]{:S(2)}) collective-permute-start(bf16[520,128]{1,0:T(8,128)(2,1)S(1)} %get-tuple-element.80), channel_id=1, source_target_pairs={{0,2},{1,3},{2,0},{3,1},{4,6},{5,7},{6,4},{7,5},{8,10},{9,11},{10,... | collective-permute-start | bytes 399368 | tf_op jit(solution)/shard_map/ppermute | solution.py:538
  169.2 7.2 %collective-permute-start.29 = (bf16[520,128]{1,0:T(8,128)(2,1)S(1)}, bf16[520,128]{1,0:T(8,128)(2,1)S(1)}, u32[]{:S(2)}, u32[]{:S(2)}) collective-permute-start(bf16[520,128]{1,0:T(8,128)(2,1)S(1)} %get-tuple-element.81), channel_id=1, source_target_pairs={{0,1},{1,0},{2,3},{3,2},{4,5},{5,4},{6,7},{7,6},{8,9},{9,8},{10,11... | collective-permute-start | bytes 399368 | tf_op jit(solution)/shard_map/ppermute | solution.py:538
  171.8 6.5 %collective-permute-start.38 = (bf16[520,128]{1,0:T(8,128)(2,1)S(1)}, bf16[520,128]{1,0:T(8,128)(2,1)S(1)}, u32[]{:S(2)}, u32[]{:S(2)}) collective-permute-start(bf16[520,128]{1,0:T(8,128)(2,1)S(1)} %get-tuple-element.92), channel_id=1, source_target_pairs={{0,12},{1,13},{2,14},{3,15},{4,8},{5,9},{6,10},{7,11},{8,4},{9,5},... | collective-permute-start | bytes 399368 | tf_op jit(solution)/shard_map/ppermute | solution.py:538
  174.6 10.2 %collective-permute-start.39 = (bf16[520,128]{1,0:T(8,128)(2,1)S(1)}, bf16[520,128]{1,0:T(8,128)(2,1)S(1)}, u32[]{:S(2)}, u32[]{:S(2)}) collective-permute-start(bf16[520,128]{1,0:T(8,128)(2,1)S(1)} %get-tuple-element.93), channel_id=1, source_target_pairs={{0,8},{1,9},{2,10},{3,11},{4,12},{5,13},{6,14},{7,15},{8,0},{9,1},... | collective-permute-start | bytes 399368 | tf_op jit(solution)/shard_map/ppermute | solution.py:538
  174.6 10.2 %collective-permute-start.40 = (bf16[520,128]{1,0:T(8,128)(2,1)S(1)}, bf16[520,128]{1,0:T(8,128)(2,1)S(1)}, u32[]{:S(2)}, u32[]{:S(2)}) collective-permute-start(bf16[520,128]{1,0:T(8,128)(2,1)S(1)} %get-tuple-element.94), channel_id=1, source_target_pairs={{0,4},{1,5},{2,6},{3,7},{4,0},{5,1},{6,2},{7,3},{8,12},{9,13},{10,... | collective-permute-start | bytes 399368 | tf_op jit(solution)/shard_map/ppermute | solution.py:538
